TPU v7x, 256 devices: a whole 4x4x8 slice. The times are simulated.
256 devices in a mesh: vir: 64 (over y, z, core), occ: 4 (over x).
Axes of the slice: x: 4, y: 4, z: 8, core: 2. Of those that a mesh axis runs over, the one named last changes fastest.
Arguments:
- tiles: float32 [4096, 128, 128], P('vir'), may hold values from -0.02734375 to 0.02734375
- tile_slot: int32 [4096], P('vir'), may hold values from 0 to 256, as said below
- amplitudes: float32 [262144, 1024], P('vir', 'occ'), may hold values from -6 to 6
- occ_energy: float32 [32], replicated, may hold values from -2 to -0.5
- vir_energy: float32 [32], replicated, may hold values from 0.5 to 3
Outputs:
- update: float32 [1024, 1024], P('vir', 'occ')
Inputs may be any that keep to these rules, and one draw needn't show every extreme that they name: `tile_slot`: for each index v of vir, the slots v * 64 to v * 64 + 63 name distinct block positions below 256, live slots first, then the empty value 8 * 32; each index has 16 or more live slots and some index has all 64 live.
All inputs are finite; a program needn't handle non-finite values.
Results may differ from a plain program's by a relative error of at most 0.0003.
Values sent between devices are 32-bit elements; how exact they have to be, the bound alone decides.
No kernel may reach another device: no remote copies, remote signals or barrier semaphores. Data moves between devices by JAX's collectives and lax.ppermute only.
A program may use at most 64 MiB of HBM per device.

v0:
```python
import jax
import jax.numpy as jnp
from jax import lax
from jax.sharding import PartitionSpec as P

NO = 32
NW = 32


def per_device(tiles, tile_slot, amplitudes, occ_energy, vir_energy):
    highest = lax.Precision.HIGHEST
    slot_count = tiles.shape[0]
    tile_size = tiles.shape[1]
    cd_dev, ij_dev = amplitudes.shape
    col_blocks = cd_dev // tile_size
    pair_rows = NW * NW
    row_blocks = pair_rows // tile_size
    occ_local = ij_dev // NO
    own_rows = pair_rows // lax.axis_size("vir")
    flat_index = lax.broadcasted_iota(jnp.int32, (row_blocks * col_blocks, slot_count), 0)
    placing = (flat_index == tile_slot[None, :]).astype(jnp.float32)
    blocks = jnp.dot(placing, tiles.reshape(slot_count, tile_size * tile_size), precision=highest)
    dense_block = blocks.reshape(row_blocks, col_blocks, tile_size, tile_size)
    dense_block = dense_block.transpose(0, 2, 1, 3).reshape(row_blocks * tile_size, cd_dev)
    partial_sum = jnp.dot(dense_block, amplitudes, precision=highest)
    swapped = partial_sum.reshape(NW, NW, ij_dev).transpose(1, 0, 2).reshape(pair_rows, ij_dev)
    direct, crossed = (
        lax.psum_scatter(partial_sum, "vir", scatter_dimension=0, tiled=True),
        lax.psum_scatter(swapped, "vir", scatter_dimension=0, tiled=True),
    )
    moved = lax.all_to_all(
        crossed.reshape(own_rows, occ_local, NO), "occ", split_axis=2, concat_axis=1, tiled=True
    )
    total = direct + moved.transpose(0, 2, 1).reshape(own_rows, ij_dev)
    row_ids = lax.axis_index("vir") * own_rows + lax.broadcasted_iota(jnp.int32, (own_rows,), 0)
    first_orb = row_ids // NW
    second_orb = row_ids % NW
    orbital = lax.broadcasted_iota(jnp.int32, (NW,), 0)
    energy_first = jnp.sum(
        jnp.where(first_orb[:, None] == orbital[None, :], vir_energy[None, :], 0.0), axis=1
    )
    energy_second = jnp.sum(
        jnp.where(second_orb[:, None] == orbital[None, :], vir_energy[None, :], 0.0), axis=1
    )
    own_occ = lax.dynamic_slice_in_dim(occ_energy, lax.axis_index("occ") * occ_local, occ_local)
    denominator = (
        own_occ[None, :, None]
        + occ_energy[None, None, :]
        - energy_first[:, None, None]
        - energy_second[:, None, None]
    )
    return (total.reshape(own_rows, occ_local, NO) / denominator).reshape(own_rows, ij_dev)


def solution(mesh):
    in_specs = (P("vir", None, None), P("vir"), P("vir", "occ"), P(), P())
    out_specs = P("vir", "occ")
    return jax.shard_map(
        per_device, mesh=mesh, in_specs=in_specs, out_specs=out_specs, check_vma=False
    )
```

profile of v0, /device:TPU:2, one launch (start us, length us, event | category | flops | bytes accessed | tf_op | source)
XLA Modules:
  0.0 333.1 jit_solution(13856259193181271727)
XLA Ops:
  6.5 0.0 reduce-scatter.5.cloned.1.call-start
  6.5 11.2 %fusion.3 = f32[8,32,128,128]{3,1,2,0:T(8,128)S(1)} fusion(s32[64]{0:T(128)} %param.6, s32[8,32]{1,0:T(8,128)S(1)} %multiply_add_fusion, f32[8,8,128,128]{3,2,1,0:T(8,128)} %bitcast.42), kind=kOutput, calls=%fused_computation.5 | convolution fusion | flops 3221241856 | bytes 20972800 | tf_op jit(solution)/shard_map/dot_general | solution.py:22
  17.7 0.0 copy-done.1
  17.8 19.5 %fusion = f32[1024,256]{1,0:T(8,128)S(1)} fusion(f32[4096,256]{1,0:T(8,128)S(1)} %copy-done.1, f32[128,8,32,128]{3,2,1,0:T(8,128)S(1)} %bitcast.40), kind=kOutput, calls=%fused_computation | convolution fusion | flops 12884901888 | bytes 22020096 | tf_op jit(solution)/shard_map/dot_general | solution.py:25
  37.2 0.0 copy-start
  37.2 0.0 copy-start.3
  37.2 0.0 copy-start.2
  37.2 1.6 copy.18
  38.9 0.0 reduce-scatter.5.cloned.1.call-update
  38.9 0.0 reduce-scatter.3.cloned.1.call-start
  39.0 0.0 copy-done
  39.0 0.7 reduce-scatter.3.cloned.1.call-update
  39.7 0.0 copy-done.3
  39.7 0.1 dynamic_slice.3
  39.8 0.0 copy-done.2
  39.8 0.2 select_reduce_fusion.1
  40.0 142.3 %reduce-scatter.5.cloned.1.call-done = f32[16,256]{1,0:T(8,128)} async-done(((f32[1024,256]{1,0:T(8,128)}), f32[16,256]{1,0:T(8,128)}) %reduce-scatter.5.cloned.1.call-update) | async-done | bytes 16400 | tf_op jit(solution)/shard_map/reduce_scatter | solution.py:29
  182.3 0.8 reshape.110
  183.1 0.1 copy.19
  183.2 0.7 reshape.121
  183.9 4.8 %all-to-all-start = ((f32[4,1,1024]{2,1,0:T(1,128)}), f32[4,1,1024]{2,1,0:T(1,128)S(1)}, u32[]{:S(2)}, u32[]{:S(2)}) async-start(f32[4,1,1024]{2,1,0:T(1,128)} %reshape.121), calls=%async_computation.2 | async-start | bytes 32768 | tf_op jit(solution)/shard_map/all_to_all | solution.py:31
  188.8 0.1 broadcast_reduce_fusion
  188.9 0.1 add.67
  188.9 0.1 add.69
  189.0 3.6 %all-to-all-done = f32[4,1,1024]{2,1,0:T(1,128)S(1)} async-done(((f32[4,1,1024]{2,1,0:T(1,128)}), f32[4,1,1024]{2,1,0:T(1,128)S(1)}, u32[]{:S(2)}, u32[]{:S(2)}) %all-to-all-start) | async-done | bytes 16416 | tf_op jit(solution)/shard_map/all_to_all | solution.py:31
  192.7 0.5 broadcast.129
  193.2 0.7 reduce.4
  193.9 0.1 reshape.122
  194.0 0.1 copy.22
  194.1 0.1 reshape.111
  194.2 130.7 %reduce-scatter.3.cloned.1.call-done = f32[16,256]{1,0:T(8,128)} async-done(((f32[1024,256]{1,0:T(8,128)}), f32[16,256]{1,0:T(8,128)}) %reduce-scatter.3.cloned.1.call-update) | async-done | bytes 16400 | tf_op jit(solution)/shard_map/reduce_scatter | solution.py:28
  324.9 1.4 subtract_divide_fusion
  (6 shorter events, 0.1 us)
Async XLA Ops:
  6.5 175.8 %reduce-scatter.5.cloned.1.call-start = ((), (), s32[]{:S(2)}) async-start(), calls=%async_computation.4 | async-start | bytes 1064960 | tf_op jit(solution)/shard_map/reduce_scatter | solution.py:29
  6.5 11.2 %copy-start.1 = (f32[4096,256]{1,0:T(8,128)S(1)}, f32[4096,256]{1,0:T(8,128)}, u32[]{:S(2)}) copy-start(f32[4096,256]{1,0:T(8,128)} %param.7) | copy-start | bytes 12582916
  37.2 1.8 copy-start
  37.2 2.5 copy-start.3
  37.2 2.5 copy-start.2
  38.9 286.0 %reduce-scatter.3.cloned.1.call-start = ((), (), s32[]{:S(2)}) async-start(), calls=%async_computation.3 | async-start | bytes 1064960 | tf_op jit(solution)/shard_map/reduce_scatter | solution.py:28
  183.9 8.7 %all-to-all-start = ((f32[4,1,1024]{2,1,0:T(1,128)}), f32[4,1,1024]{2,1,0:T(1,128)S(1)}, u32[]{:S(2)}, u32[]{:S(2)}) async-start(f32[4,1,1024]{2,1,0:T(1,128)} %reshape.121), calls=%async_computation.2 | async-start | bytes 32768 | tf_op jit(solution)/shard_map/all_to_all | solution.py:31
Sparse Core Ops, SparseCore 0:
  39.0 143.2 reduce-scatter.4
  186.3 138.5 reduce-scatter.2
where the time goes:
time: 334 us; the launch traced here: 333 us
  waiting for transfers between devices  277 us (83%)
  matrix products  30.6 us (9%)
  between operations  13.5 us (4%)
  starting transfers between devices  4.87 us (1%)
  local copies, waits for them, and re-layouts  4.44 us (1%)
    reduce_scatter x1, waiting for transfers between devices, per_device(): lax.psum_scatter(swapped, 'vir', scatter_dimension=0, tiled=True)  142 us
    reduce_scatter x1, waiting for transfers between devices, per_device(): lax.psum_scatter(partial_sum, 'vir', scatter_dimension=0, tiled=True)  131 us
    dot_general x1, matrix products, per_device(): partial_sum = jnp.dot(dense_block, amplitudes, precision=highest)  19.5 us
    dot_general x1, matrix products, per_device(): jnp.dot(placing, tiles.reshape(slot_count, tile_size * tile_size), precis...  11.2 us
  transfers between devices with their start and end apart: 3, of which 3 were waited for; matrix products, arithmetic and copies ran while one was open for 1% of the time, Pallas kernels for 0%

commit v1 on v0

v1 whole, which is shorter than its diff:
```python
import functools

import jax
import jax.numpy as jnp
from jax import lax
from jax.experimental import pallas as pl
from jax.experimental.pallas import tpu as pltpu
from jax.sharding import Mesh
from jax.sharding import PartitionSpec as P

F32 = jnp.float32
BF16 = jnp.bfloat16
TILE = 128
CAP = 64
COLS = 32
CHUNKS = 8
NY, NZ, NX = 4, 8, 4
HALF = 16
VIR = ("y", "z", "core")


def vmem_spec():
    return pl.BlockSpec(memory_space=pltpu.VMEM)


def split3(x):
    top = x.astype(BF16)
    rest = x - top.astype(F32)
    mid = rest.astype(BF16)
    low = (rest - mid.astype(F32)).astype(BF16)
    return top, mid, low


def permute_lanes(x, place):
    top, mid, low = split3(x)
    out = jnp.dot(low, place, preferred_element_type=F32)
    out = out + jnp.dot(mid, place, preferred_element_type=F32)
    return out + jnp.dot(top, place, preferred_element_type=F32)


def ladder_kernel(slot_ref, pos_ref, tiles_hbm, amps_hbm, keep_ref, send_ref, tbuf, abuf, stack, acc, tsem, asem):
    arows, trows = abuf.shape[0] // CHUNKS, CAP // CHUNKS

    def amp_copy(c):
        rows = pl.ds(c * arows, arows)
        return pltpu.make_async_copy(amps_hbm.at[rows], abuf.at[rows], asem.at[c])

    def tile_copy(c):
        rows = pl.ds(c * trows, trows)
        return pltpu.make_async_copy(tiles_hbm.at[rows], tbuf.at[rows], tsem.at[c])

    for c in range(CHUNKS):
        amp_copy(c).start()
    for c in range(CHUNKS):
        tile_copy(c).start()
    acc[...] = jnp.zeros_like(acc)
    for c in range(CHUNKS):
        amp_copy(c).wait()

        @pl.loop(0, arows // TILE)
        def _(q, c=c):
            block = c * (arows // TILE) + q
            a = abuf[pl.ds(pl.multiple_of(block * TILE, TILE), TILE), :]
            top = a.astype(BF16)
            stack[block, 0:TILE, :] = top
            stack[block, TILE : 2 * TILE, :] = (a - top.astype(F32)).astype(BF16)

    @pl.loop(0, CHUNKS)
    def _(c):
        tile_copy(c).wait()
        for u in range(trows):
            slot = slot_ref[c * trows + u]
            row = pl.multiple_of((slot // COLS) * TILE, TILE)
            col = slot % COLS
            t = tbuf[c * trows + u]
            top = t.astype(BF16)
            low = (t - top.astype(F32)).astype(BF16)
            part = jnp.dot(jnp.concatenate([top, top], axis=1), stack[col], preferred_element_type=F32)
            part = part + jnp.dot(low, stack[col, 0:TILE, :], preferred_element_type=F32)
            acc[pl.ds(row, TILE), :] += part

    s = pos_ref[0]
    for a in range(32):
        b_high = (a // HALF + s) % 2
        rows = pl.ds(a * HALF, HALF)
        keep_ref[rows, :] = acc[pl.ds(pl.multiple_of(a * 32 + b_high * HALF, HALF), HALF), :]
        send_ref[rows, :] = acc[pl.ds(pl.multiple_of(a * 32 + (1 - b_high) * HALF, HALF), HALF), :]


def split_kernel(pos_ref, keep_ref, recv_ref, direct_ref, own_ref, p1_ref, p2_ref, p3_ref, xbuf, pieces):
    n = lax.broadcasted_iota(jnp.int32, (256, 256), 0)
    g = lax.broadcasted_iota(jnp.int32, (256, 256), 1)
    base = 8 * (g // 64)
    mid = (g // 8) % 8
    low = g % 8
    place = (n == mid * 32 + base + low).astype(F32).astype(BF16)
    turned = (n == low * 32 + base + mid).astype(F32).astype(BF16)
    total = keep_ref[...] + recv_ref[...]
    direct_ref[...] = permute_lanes(total, place)
    mirrored = permute_lanes(total, turned)
    for t in range(2):
        xbuf[t] = mirrored[:, t * 128 : t * 128 + 128]
    s, x = pos_ref[0], pos_ref[1]
    left = lax.broadcasted_iota(jnp.int32, (HALF, 128), 1) < 64
    for a in range(HALF):
        rows = pl.ds(a * HALF, HALF)
        for t in range(2):
            one = xbuf[t, pl.ds(s * 256 + a, HALF, stride=HALF), :]
            two = xbuf[t, pl.ds((1 - s) * 256 + a, HALF, stride=HALF), :]
            pieces[2 * t, rows, :] = jnp.where(left, one, pltpu.roll(two, 64, 1))
            pieces[2 * t + 1, rows, :] = jnp.where(left, pltpu.roll(one, 64, 1), two)
    for k, ref in enumerate((own_ref, p1_ref, p2_ref, p3_ref)):
        ref[...] = pieces[lax.rem(x + k, NX)]


def mirror_kernel(pos_ref, direct_ref, own_ref, q1_ref, q2_ref, q3_ref, o0_ref, o1_ref, o2_ref, o3_ref, pieces, total):
    x, y = pos_ref[1], pos_ref[2]
    for k, ref in enumerate((own_ref, q1_ref, q2_ref, q3_ref)):
        pieces[lax.rem(x + NX - k, NX)] = ref[...]
    left = lax.broadcasted_iota(jnp.int32, (256, 128), 1) < 64
    for t in range(2):
        even, odd = pieces[2 * t], pieces[2 * t + 1]
        lanes = pl.ds(t * 128, 128)
        total[0:256, lanes] = direct_ref[0:256, lanes] + jnp.where(left, even, pltpu.roll(odd, 64, 1))
        total[256:512, lanes] = direct_ref[256:512, lanes] + jnp.where(left, pltpu.roll(even, 64, 1), odd)
    for k, ref in enumerate((o0_ref, o1_ref, o2_ref, o3_ref)):
        ref[...] = total[pl.ds(pl.multiple_of(lax.rem(y + k, NY) * 128, 128), 128), :]


def finish_kernel(parts_ref, denom_ref, out_ref):
    n = lax.broadcasted_iota(jnp.int32, (256, 256), 1)
    g = lax.broadcasted_iota(jnp.int32, (256, 256), 0)
    back = (n == ((g // 8) % 8) * 32 + 8 * (g // 64) + g % 8).astype(F32).astype(BF16)
    total = parts_ref[0]
    for z in range(1, NZ):
        total = total + parts_ref[z]
    out_ref[...] = permute_lanes(total, back) / denom_ref[...]


def params(mib):
    return pltpu.CompilerParams(vmem_limit_bytes=mib << 20)


def f32(*shape):
    return jax.ShapeDtypeStruct(shape, F32)


def shift_y(k):
    pairs = []
    for y in range(NY):
        to = (y + k) % NY
        for z in range(NZ):
            for core in range(2):
                core_to = core ^ (y >= 2) ^ (to >= 2)
                pairs.append(((y * NZ + z) * 2 + core, (to * NZ + z) * 2 + core_to))
    return pairs


def shift_x(k):
    return [(x, (x + k) % NX) for x in range(NX)]


def per_device(tiles, tile_slot, amplitudes, occ_energy, vir_energy):
    y, z, core, x = (lax.axis_index(name) for name in ("y", "z", "core", "occ"))
    s = lax.bitwise_xor(core, (y >= 2).astype(core.dtype))
    pos = jnp.stack([s, x, y]).astype(jnp.int32)
    smem = pl.BlockSpec(memory_space=pltpu.SMEM)
    keep, send = pl.pallas_call(
        ladder_kernel,
        in_specs=[smem, smem] + [pl.BlockSpec(memory_space=pltpu.HBM)] * 2,
        out_specs=[vmem_spec()] * 2,
        out_shape=[f32(512, 256)] * 2,
        scratch_shapes=[
            pltpu.VMEM((CAP, TILE, TILE), F32),
            pltpu.VMEM((COLS * TILE, 256), F32),
            pltpu.VMEM((COLS, 2 * TILE, 256), BF16),
            pltpu.VMEM((1024 + TILE, 256), F32),
            pltpu.SemaphoreType.DMA((CHUNKS,)),
            pltpu.SemaphoreType.DMA((CHUNKS,)),
        ],
        compiler_params=params(24),
        name="ladder",
    )(tile_slot, pos, tiles, amplitudes)
    recv = lax.ppermute(send, "core", [(0, 1), (1, 0)])
    direct, *pieces = pl.pallas_call(
        split_kernel,
        in_specs=[smem] + [vmem_spec()] * 2,
        out_specs=[vmem_spec()] * 5,
        out_shape=[f32(512, 256)] + [f32(256, 128)] * 4,
        scratch_shapes=[pltpu.VMEM((2, 512, 128), F32), pltpu.VMEM((4, 256, 128), F32)],
        compiler_params=params(16),
        name="split",
    )(pos, keep, recv)
    moved = [lax.ppermute(pieces[k], "occ", shift_x(k)) for k in range(1, NX)]
    own, *others = pl.pallas_call(
        mirror_kernel,
        in_specs=[smem] + [vmem_spec()] * 5,
        out_specs=[vmem_spec()] * 4,
        out_shape=[f32(128, 256)] * 4,
        scratch_shapes=[pltpu.VMEM((4, 256, 128), F32), pltpu.VMEM((512, 256), F32)],
        compiler_params=params(16),
        name="mirror",
    )(pos, direct, pieces[0], *moved)
    for k in range(1, NY):
        own = own + lax.ppermute(others[k - 1], VIR, shift_y(k))
    parts = lax.all_to_all(own.reshape(NZ, HALF, 256), "z", 0, 0)

    def pick(table, index):
        orbital = lax.broadcasted_iota(jnp.int32, (index.shape[0], 32), 1)
        return jnp.sum(jnp.where(index[:, None] == orbital, table[None, :], 0.0), axis=1)

    n = lax.broadcasted_iota(jnp.int32, (256,), 0)
    row = lax.broadcasted_iota(jnp.int32, (HALF,), 0)
    pair = pick(occ_energy, x * 8 + n // 32) + pick(occ_energy, n % 32)
    first = pick(vir_energy, jnp.full((HALF,), y * NZ + z, jnp.int32))
    second = pick(vir_energy, core * HALF + row)
    denominator = pair[None, :] - first[:, None] - second[:, None]
    return pl.pallas_call(
        finish_kernel,
        in_specs=[vmem_spec()] * 2,
        out_specs=vmem_spec(),
        out_shape=f32(HALF, 256),
        compiler_params=params(16),
        name="finish",
    )(parts, denominator)


def solution(mesh):
    fine = Mesh(mesh.devices.reshape(NY, NZ, 2, NX), ("y", "z", "core", "occ"))
    in_specs = (P(VIR, None, None), P(VIR), P(VIR, "occ"), P(), P())
    return jax.shard_map(
        per_device, mesh=fine, in_specs=in_specs, out_specs=P(VIR, "occ"), check_vma=False
    )
```

time: 334 us -> 55.9 us (0.17)
  waiting for transfers between devices: 277 us -> 23.1 us
  matrix products: 30.6 us -> 0 us
  between operations: 13.5 us -> 0.06 us
  starting transfers between devices: 4.87 us -> 17.2 us
  Pallas kernels: 0 us -> 8.78 us
    reduce_scatter x2 -> x0, waiting for transfers between devices: 273 us -> none  [the longest x1 142 us: per_device(): lax.psum_scatter(swapped, 'vir', scatter_dimension=0, tiled=True)]
    dot_general x2 -> x0, matrix products: 30.6 us -> none  [the longest x1 19.5 us: per_device(): partial_sum = jnp.dot(dense_block, amplitudes, precision=highest)]
    ppermute x0 -> x7, waiting for transfers between devices: none -> 14.3 us  [the longest x3 6.28 us: per_device(): moved = [lax.ppermute(pieces[k], 'occ', shift_x(k)) for k in range(1, NX)]]
    ppermute x0 -> x7, starting transfers between devices: none -> 8.83 us  [the longest x3 4.84 us: per_device(): moved = [lax.ppermute(pieces[k], 'occ', shift_x(k)) for k in range(1, NX)]]
    pallas_call x0 -> x4, Pallas kernels: none -> 8.78 us  [the longest x1 5.66 us: per_device(): pl.pallas_call(ladder_kernel, in_specs=[smem, smem] + [pl.BlockSpec(memor...]
    all_to_all x1, waiting for transfers between devices: 3.65 us -> 8.81 us  [per_device(): parts = lax.all_to_all(own.reshape(NZ, HALF, 256), 'z', 0, 0)]
    unnamed x10, local copies, waits for them, and re-layouts: 0.84 us -> 5.04 us
    all_to_all x1, starting transfers between devices: 4.83 us -> 8.33 us  [per_device(): parts = lax.all_to_all(own.reshape(NZ, HALF, 256), 'z', 0, 0)]
  transfers between devices with their start and end apart: 3 -> 8, of which waited for: 3 -> 7; matrix products, arithmetic and copies ran while one was open for 1% -> 1% of each run, Pallas kernels for 0% -> 0%
where the time goes in v1:
time: 55.9 us; the launch traced here: 55.3 us
  waiting for transfers between devices  23.1 us (41%)
  starting transfers between devices  17.2 us (31%)
  Pallas kernels  8.78 us (16%)
  local copies, waits for them, and re-layouts  5.04 us (9%)
  other arithmetic  1.12 us (2%)
    all_to_all x1, waiting for transfers between devices, per_device(): parts = lax.all_to_all(own.reshape(NZ, HALF, 256), 'z', 0, 0)  8.81 us
    all_to_all x1, starting transfers between devices, per_device(): parts = lax.all_to_all(own.reshape(NZ, HALF, 256), 'z', 0, 0)  8.33 us
    ppermute x3, waiting for transfers between devices, per_device(): moved = [lax.ppermute(pieces[k], 'occ', shift_x(k)) for k in range(1, NX)]  6.28 us
    ppermute x3, waiting for transfers between devices, per_device(): own = own + lax.ppermute(others[k - 1], VIR, shift_y(k))  6.11 us
    pallas_call x1, Pallas kernels, per_device(): pl.pallas_call(ladder_kernel, in_specs=[smem, smem] + [pl.BlockSpec(memor...  5.66 us
    unnamed x10, local copies, waits for them, and re-layouts  5.04 us
    ppermute x3, starting transfers between devices, per_device(): moved = [lax.ppermute(pieces[k], 'occ', shift_x(k)) for k in range(1, NX)]  4.84 us
    ppermute x3, starting transfers between devices, per_device(): own = own + lax.ppermute(others[k - 1], VIR, shift_y(k))  3.9 us
  transfers between devices with their start and end apart: 8, of which 7 were waited for; matrix products, arithmetic and copies ran while one was open for 1% of the time, Pallas kernels for 0%

profile of v1, /device:TPU:2, one launch (start us, length us, event | category | flops | bytes accessed | tf_op | source)
XLA Modules:
  0.0 55.3 jit_solution(7337610962210687466)
XLA Ops:
  0.0 0.1 pad_add_fusion.pos_ref
  0.1 0.0 copy-start
  0.1 2.2 %copy-done = f32[64,128,128]{2,1,0:T(8,128)S(1)} copy-done((f32[64,128,128]{2,1,0:T(8,128)S(1)}, f32[64,128,128]{2,1,0:T(8,128)}, u32[]{:S(2)}) %copy-start) | copy-done | bytes 4194328
  2.3 0.0 copy-start.1
  2.3 2.2 %copy-done.1 = f32[4096,256]{1,0:T(8,128)S(1)} copy-done((f32[4096,256]{1,0:T(8,128)S(1)}, f32[4096,256]{1,0:T(8,128)}, u32[]{:S(2)}) %copy-start.1) | copy-done | bytes 4194328
  4.5 0.7 %copy-done.2 = s32[64]{0:T(128)S(1)} copy-done((s32[64]{0:T(128)S(1)}, s32[64]{0:T(128)}, u32[]{:S(2)}) %copy-start.2) | copy-done | bytes 280
  5.1 5.7 %ladder.1 = (f32[512,256]{1,0:T(8,128)S(1)}, f32[512,256]{1,0:T(8,128)S(1)}) custom-call(s32[64]{0:T(128)S(1)} %copy-done.2, s32[3]{0:T(128)S(1)} %pad_add_fusion.pos_ref, f32[64,128,128]{2,1,0:T(8,128)S(1)} %copy-done, f32[4096,256]{1,0:T(8,128)S(1)} %copy-done.1), custom_call_target="tpu_custom_call" | custom-call | tf_op jit(solution)/shard_map/ladder/pallas_call | solution.py:168
  10.8 0.1 collective-permute-start
  10.9 1.9 %collective-permute-done.recv_ref = f32[512,256]{1,0:T(8,128)S(1)} collective-permute-done((f32[512,256]{1,0:T(8,128)S(1)}, f32[512,256]{1,0:T(8,128)S(1)}, u32[]{:S(2)}, u32[]{:S(2)}) %collective-permute-start) | collective-permute-done | bytes 524320 | tf_op jit(solution)/shard_map/ppermute | solution.py:184
  12.8 1.4 %split.1 = (f32[512,256]{1,0:T(8,128)S(1)}, f32[256,128]{1,0:T(8,128)S(1)}, f32[256,128]{1,0:T(8,128)S(1)}, f32[256,128]{1,0:T(8,128)S(1)}, f32[256,128]{1,0:T(8,128)S(1)}) custom-call(s32[3]{0:T(128)S(1)} %pad_add_fusion.pos_ref, f32[512,256]{1,0:T(8,128)S(1)} %get-tuple-element.16.keep_ref, f32[512,256]{1,0:T(8,128)S(1)} %collective-permute-done.recv_ref), custom_call_target="tpu_custom_call" | custom-call | tf_op jit(solution)/shard_map/split/pallas_call | solution.py:185
  14.2 1.6 %collective-permute-start.1 = (f32[256,128]{1,0:T(8,128)S(1)}, f32[256,128]{1,0:T(8,128)S(1)}, u32[]{:S(2)}, u32[]{:S(2)}) collective-permute-start(f32[256,128]{1,0:T(8,128)S(1)} %get-tuple-element.20), channel_id=1, source_target_pairs={{0,1},{1,2},{2,3},{3,0},{4,5},{5,6},{6,7},{7,4},{8,9},{9,10},{10,1... | collective-permute-start | bytes 393224 | tf_op jit(solution)/shard_map/ppermute | solution.py:194
  15.8 2.8 %collective-permute-start.2 = (f32[256,128]{1,0:T(8,128)S(1)}, f32[256,128]{1,0:T(8,128)S(1)}, u32[]{:S(2)}, u32[]{:S(2)}) collective-permute-start(f32[256,128]{1,0:T(8,128)S(1)} %get-tuple-element.21), channel_id=1, source_target_pairs={{0,2},{1,3},{2,0},{3,1},{4,6},{5,7},{6,4},{7,5},{8,10},{9,11},{10,... | collective-permute-start | bytes 393224 | tf_op jit(solution)/shard_map/ppermute | solution.py:194
  18.6 0.5 collective-permute-start.3
  19.1 1.8 %collective-permute-done.1.q1_ref = f32[256,128]{1,0:T(8,128)S(1)} collective-permute-done((f32[256,128]{1,0:T(8,128)S(1)}, f32[256,128]{1,0:T(8,128)S(1)}, u32[]{:S(2)}, u32[]{:S(2)}) %collective-permute-start.1) | collective-permute-done | bytes 131104 | tf_op jit(solution)/shard_map/ppermute | solution.py:194
  20.9 2.8 %collective-permute-done.2.q2_ref = f32[256,128]{1,0:T(8,128)S(1)} collective-permute-done((f32[256,128]{1,0:T(8,128)S(1)}, f32[256,128]{1,0:T(8,128)S(1)}, u32[]{:S(2)}, u32[]{:S(2)}) %collective-permute-start.2) | collective-permute-done | bytes 131104 | tf_op jit(solution)/shard_map/ppermute | solution.py:194
  23.7 1.7 %collective-permute-done.3.q3_ref = f32[256,128]{1,0:T(8,128)S(1)} collective-permute-done((f32[256,128]{1,0:T(8,128)S(1)}, f32[256,128]{1,0:T(8,128)S(1)}, u32[]{:S(2)}, u32[]{:S(2)}) %collective-permute-start.3) | collective-permute-done | bytes 131104 | tf_op jit(solution)/shard_map/ppermute | solution.py:194
  25.4 0.8 %mirror.1 = (f32[128,256]{1,0:T(8,128)S(1)}, f32[128,256]{1,0:T(8,128)S(1)}, f32[128,256]{1,0:T(8,128)S(1)}, f32[128,256]{1,0:T(8,128)S(1)}) custom-call(s32[3]{0:T(128)S(1)} %pad_add_fusion.pos_ref, f32[512,256]{1,0:T(8,128)S(1)} %get-tuple-element.18.direct_ref, f32[256,128]{1,0:T(8,128)S(1)} %get-tuple-element.19.own_ref, ...), custom_call_target="tpu_custom_call" | custom-call | tf_op jit(solution)/shard_map/mirror/pallas_call | solution.py:195
  26.2 1.0 %collective-permute-start.4 = (f32[128,256]{1,0:T(8,128)S(1)}, f32[128,256]{1,0:T(8,128)S(1)}, u32[]{:S(2)}, u32[]{:S(2)}) collective-permute-start(f32[128,256]{1,0:T(8,128)S(1)} %get-tuple-element.24), channel_id=1, source_target_pairs={{0,64},{4,68},{8,72},{12,76},{16,80},{20,84},{24,88},{28,92},{32,9... | collective-permute-start | bytes 393224 | tf_op jit(solution)/shard_map/ppermute | solution.py:205
  27.2 1.6 %collective-permute-start.5 = (f32[128,256]{1,0:T(8,128)S(1)}, f32[128,256]{1,0:T(8,128)S(1)}, u32[]{:S(2)}, u32[]{:S(2)}) collective-permute-start(f32[128,256]{1,0:T(8,128)S(1)} %get-tuple-element.25), channel_id=1, source_target_pairs={{0,132},{4,128},{8,140},{12,136},{16,148},{20,144},{24,156},{28,15... | collective-permute-start | bytes 393224 | tf_op jit(solution)/shard_map/ppermute | solution.py:205
  28.8 1.3 %collective-permute-start.6 = (f32[128,256]{1,0:T(8,128)S(1)}, f32[128,256]{1,0:T(8,128)S(1)}, u32[]{:S(2)}, u32[]{:S(2)}) collective-permute-start(f32[128,256]{1,0:T(8,128)S(1)} %get-tuple-element.26), channel_id=1, source_target_pairs={{0,196},{4,192},{8,204},{12,200},{16,212},{20,208},{24,220},{28,21... | collective-permute-start | bytes 393224 | tf_op jit(solution)/shard_map/ppermute | solution.py:205
  30.1 0.0 copy-done.3
  30.1 0.1 select_reduce_fusion
  30.2 5.8 %collective-permute-done.4 = f32[128,256]{1,0:T(8,128)S(1)} collective-permute-done((f32[128,256]{1,0:T(8,128)S(1)}, f32[128,256]{1,0:T(8,128)S(1)}, u32[]{:S(2)}, u32[]{:S(2)}) %collective-permute-start.4) | collective-permute-done | bytes 131104 | tf_op jit(solution)/shard_map/ppermute | solution.py:205
  36.1 0.0 collective-permute-done.5
  36.1 0.3 collective-permute-done.6
  36.3 0.7 %add_add_fusion = f32[128,256]{1,0:T(8,128)} fusion(f32[128,256]{1,0:T(8,128)S(1)} %collective-permute-done.6, f32[128,256]{1,0:T(8,128)S(1)} %collective-permute-done.5, f32[128,256]{1,0:T(8,128)S(1)} %get-tuple-element.23, f32[128,256]{1,0:T(8,128)S(1)} %collective-permute-done.4), kind=kLoop, calls=%fused_computation | loop fusion | flops 98304 | bytes 655360 | tf_op jit(solution)/shard_map/add | solution.py:205
  37.0 8.3 %all-to-all-start = ((f32[8,16,256]{2,1,0:T(8,128)}), f32[8,16,256]{2,1,0:T(8,128)S(1)}, u32[]{:S(2)}, u32[]{:S(2)}) async-start(f32[8,16,256]{2,1,0:T(8,128)} %bitcast.3), calls=%async_computation | async-start | bytes 262144 | tf_op jit(solution)/shard_map/all_to_all | solution.py:206
  45.4 0.0 copy-done.4
  45.4 0.2 select_reduce_fusion.3
  45.5 0.1 subtract_subtract_fusion.denom_ref
  45.6 8.8 %all-to-all-done.parts_ref = f32[8,16,256]{2,1,0:T(8,128)S(1)} async-done(((f32[8,16,256]{2,1,0:T(8,128)}), f32[8,16,256]{2,1,0:T(8,128)S(1)}, u32[]{:S(2)}, u32[]{:S(2)}) %all-to-all-start) | async-done | bytes 131104 | tf_op jit(solution)/shard_map/all_to_all | solution.py:206
  54.4 0.8 %finish.1 = f32[16,256]{1,0:T(8,128)} custom-call(f32[8,16,256]{2,1,0:T(8,128)S(1)} %all-to-all-done.parts_ref, f32[16,256]{1,0:T(8,128)S(1)} %subtract_subtract_fusion.denom_ref), custom_call_target="tpu_custom_call" | custom-call | tf_op jit(solution)/shard_map/finish/pallas_call | solution.py:218
  (7 shorter events, 0.0 us)
Async XLA Ops:
  0.1 2.2 %copy-start = (f32[64,128,128]{2,1,0:T(8,128)S(1)}, f32[64,128,128]{2,1,0:T(8,128)}, u32[]{:S(2)}) copy-start(f32[64,128,128]{2,1,0:T(8,128)} %tiles_hbm.1) | copy-start | bytes 12582916
  2.3 2.2 %copy-start.1 = (f32[4096,256]{1,0:T(8,128)S(1)}, f32[4096,256]{1,0:T(8,128)}, u32[]{:S(2)}) copy-start(f32[4096,256]{1,0:T(8,128)} %amps_hbm.1) | copy-start | bytes 12582916
  4.5 0.7 %copy-start.2 = (s32[64]{0:T(128)S(1)}, s32[64]{0:T(128)}, u32[]{:S(2)}) copy-start(s32[64]{0:T(128)} %slot_ref.1) | copy-start | bytes 772
  5.1 25.0 %copy-start.3 = (f32[32]{0:T(128)S(1)}, f32[32]{0:T(128)}, u32[]{:S(2)}) copy-start(f32[32]{0:T(128)} %param.8) | copy-start | bytes 388
  5.1 40.2 %copy-start.4 = (f32[32]{0:T(128)S(1)}, f32[32]{0:T(128)}, u32[]{:S(2)}) copy-start(f32[32]{0:T(128)} %param.9) | copy-start | bytes 388
  10.8 2.0 %collective-permute-start = (f32[512,256]{1,0:T(8,128)S(1)}, f32[512,256]{1,0:T(8,128)S(1)}, u32[]{:S(2)}, u32[]{:S(2)}) collective-permute-start(f32[512,256]{1,0:T(8,128)S(1)} %get-tuple-element.17), channel_id=1, source_target_pairs={{0,4},{4,0},{1,5},{5,1},{2,6},{6,2},{3,7},{7,3},{8,12},{12,8},{9,1... | collective-permute-start | bytes 1572872 | tf_op jit(solution)/shard_map/ppermute | solution.py:184
  14.2 6.7 %collective-permute-start.1 = (f32[256,128]{1,0:T(8,128)S(1)}, f32[256,128]{1,0:T(8,128)S(1)}, u32[]{:S(2)}, u32[]{:S(2)}) collective-permute-start(f32[256,128]{1,0:T(8,128)S(1)} %get-tuple-element.20), channel_id=1, source_target_pairs={{0,1},{1,2},{2,3},{3,0},{4,5},{5,6},{6,7},{7,4},{8,9},{9,10},{10,1... | collective-permute-start | bytes 393224 | tf_op jit(solution)/shard_map/ppermute | solution.py:194
  15.8 7.9 %collective-permute-start.2 = (f32[256,128]{1,0:T(8,128)S(1)}, f32[256,128]{1,0:T(8,128)S(1)}, u32[]{:S(2)}, u32[]{:S(2)}) collective-permute-start(f32[256,128]{1,0:T(8,128)S(1)} %get-tuple-element.21), channel_id=1, source_target_pairs={{0,2},{1,3},{2,0},{3,1},{4,6},{5,7},{6,4},{7,5},{8,10},{9,11},{10,... | collective-permute-start | bytes 393224 | tf_op jit(solution)/shard_map/ppermute | solution.py:194
  18.6 6.8 %collective-permute-start.3 = (f32[256,128]{1,0:T(8,128)S(1)}, f32[256,128]{1,0:T(8,128)S(1)}, u32[]{:S(2)}, u32[]{:S(2)}) collective-permute-start(f32[256,128]{1,0:T(8,128)S(1)} %get-tuple-element.22), channel_id=1, source_target_pairs={{0,3},{1,0},{2,1},{3,2},{4,7},{5,4},{6,5},{7,6},{8,11},{9,8},{10,9... | collective-permute-start | bytes 393224 | tf_op jit(solution)/shard_map/ppermute | solution.py:194
  26.2 9.8 %collective-permute-start.4 = (f32[128,256]{1,0:T(8,128)S(1)}, f32[128,256]{1,0:T(8,128)S(1)}, u32[]{:S(2)}, u32[]{:S(2)}) collective-permute-start(f32[128,256]{1,0:T(8,128)S(1)} %get-tuple-element.24), channel_id=1, source_target_pairs={{0,64},{4,68},{8,72},{12,76},{16,80},{20,84},{24,88},{28,92},{32,9... | collective-permute-start | bytes 393224 | tf_op jit(solution)/shard_map/ppermute | solution.py:205
  27.2 8.8 %collective-permute-start.5 = (f32[128,256]{1,0:T(8,128)S(1)}, f32[128,256]{1,0:T(8,128)S(1)}, u32[]{:S(2)}, u32[]{:S(2)}) collective-permute-start(f32[128,256]{1,0:T(8,128)S(1)} %get-tuple-element.25), channel_id=1, source_target_pairs={{0,132},{4,128},{8,140},{12,136},{16,148},{20,144},{24,156},{28,15... | collective-permute-start | bytes 393224 | tf_op jit(solution)/shard_map/ppermute | solution.py:205
  28.8 7.6 %collective-permute-start.6 = (f32[128,256]{1,0:T(8,128)S(1)}, f32[128,256]{1,0:T(8,128)S(1)}, u32[]{:S(2)}, u32[]{:S(2)}) collective-permute-start(f32[128,256]{1,0:T(8,128)S(1)} %get-tuple-element.26), channel_id=1, source_target_pairs={{0,196},{4,192},{8,204},{12,200},{16,212},{20,208},{24,220},{28,21... | collective-permute-start | bytes 393224 | tf_op jit(solution)/shard_map/ppermute | solution.py:205
  37.0 17.4 %all-to-all-start = ((f32[8,16,256]{2,1,0:T(8,128)}), f32[8,16,256]{2,1,0:T(8,128)S(1)}, u32[]{:S(2)}, u32[]{:S(2)}) async-start(f32[8,16,256]{2,1,0:T(8,128)} %bitcast.3), calls=%async_computation | async-start | bytes 262144 | tf_op jit(solution)/shard_map/all_to_all | solution.py:206

commit v2 on v1

v2 whole, which is shorter than its diff:
```python
import functools

import jax
import jax.numpy as jnp
from jax import lax
from jax.experimental import pallas as pl
from jax.experimental.pallas import tpu as pltpu
from jax.sharding import Mesh
from jax.sharding import PartitionSpec as P

F32 = jnp.float32
BF16 = jnp.bfloat16
TILE = 128
CAP = 64
COLS = 32
CHUNKS = 8
NY, NZ, NX = 4, 8, 4
HALF = 16
EIGHT = 8
VIR = ("y", "z", "core")


def vmem_spec():
    return pl.BlockSpec(memory_space=pltpu.VMEM)


def split3(x):
    top = x.astype(BF16)
    rest = x - top.astype(F32)
    mid = rest.astype(BF16)
    low = (rest - mid.astype(F32)).astype(BF16)
    return top, mid, low


def permute_lanes(x, place):
    top, mid, low = split3(x)
    out = jnp.dot(low, place, preferred_element_type=F32)
    out = out + jnp.dot(mid, place, preferred_element_type=F32)
    return out + jnp.dot(top, place, preferred_element_type=F32)


def row_set(y, core):
    return lax.bitwise_xor(core, (y >= NY // 2).astype(jnp.int32))


def place(name):
    return lax.axis_index(name).astype(jnp.int32)


def ladder_kernel(slot_hbm, tiles_hbm, amps_hbm, *rest):
    outs, (slots, tbuf, abuf, stack, acc, ssem, tsem, asem) = rest[:2], rest[2:]
    arows, trows = abuf.shape[0] // CHUNKS, CAP // CHUNKS

    def amp_copy(c):
        rows = pl.ds(c * arows, arows)
        return pltpu.make_async_copy(amps_hbm.at[rows], abuf.at[rows], asem.at[c])

    def tile_copy(c):
        rows = pl.ds(c * trows, trows)
        return pltpu.make_async_copy(tiles_hbm.at[rows], tbuf.at[rows], tsem.at[c])

    slot_copy = pltpu.make_async_copy(slot_hbm, slots, ssem)
    slot_copy.start()
    for c in range(CHUNKS):
        amp_copy(c).start()
    for c in range(CHUNKS):
        tile_copy(c).start()
    acc[...] = jnp.zeros_like(acc)

    @pl.loop(0, CHUNKS)
    def _(c):
        amp_copy(c).wait()
        for q in range(arows // TILE):
            block = c * (arows // TILE) + q
            a = abuf[pl.ds(pl.multiple_of(block * TILE, TILE), TILE), :]
            top = a.astype(BF16)
            stack[block, 0:TILE, :] = top
            stack[block, TILE : 2 * TILE, :] = (a - top.astype(F32)).astype(BF16)

    slot_copy.wait()

    @pl.loop(0, CHUNKS)
    def _(c):
        tile_copy(c).wait()
        for u in range(trows):
            slot = slots[c * trows + u]
            row = pl.multiple_of((slot // COLS) * TILE, TILE)
            col = slot % COLS
            t = tbuf[c * trows + u]
            top = t.astype(BF16)
            low = (t - top.astype(F32)).astype(BF16)
            part = jnp.dot(jnp.concatenate([top, top], axis=1), stack[col], preferred_element_type=F32)
            part = part + jnp.dot(low, stack[col, 0:TILE, :], preferred_element_type=F32)
            acc[pl.ds(row, TILE), :] += part

    s = row_set(place("y"), place("core"))
    for a in range(32):
        for own in range(2):
            b_high = (a // HALF + s + own) % 2
            row = pl.multiple_of(a * 32 + b_high * HALF, HALF)
            outs[own][pl.ds(a * HALF, HALF), :] = acc[pl.ds(row, HALF), :]


def column_order(turned):
    n = lax.broadcasted_iota(jnp.int32, (256, 256), 0)
    g = lax.broadcasted_iota(jnp.int32, (256, 256), 1)
    outer, inner = (g // EIGHT) % EIGHT, g % EIGHT
    if turned:
        outer, inner = inner, outer
    return (n == outer * 32 + EIGHT * (g // 64) + inner).astype(F32).astype(BF16)


def split_kernel(keep_ref, recv_ref, own_ref, p1_ref, p2_ref, p3_ref, xbuf, pieces):
    mirrored = permute_lanes(keep_ref[...] + recv_ref[...], column_order(True))
    for t in range(2):
        xbuf[t] = mirrored[:, t * 128 : t * 128 + 128]
    s, x = row_set(place("y"), place("core")), place("occ")
    left = lax.broadcasted_iota(jnp.int32, (HALF, 128), 1) < 64
    for a in range(HALF):
        rows = pl.ds(a * HALF, HALF)
        for t in range(2):
            one = xbuf[t, pl.ds(s * 256 + a, HALF, stride=HALF), :]
            two = xbuf[t, pl.ds((1 - s) * 256 + a, HALF, stride=HALF), :]
            pieces[2 * t, rows, :] = jnp.where(left, one, pltpu.roll(two, 64, 1))
            pieces[2 * t + 1, rows, :] = jnp.where(left, pltpu.roll(one, 64, 1), two)
    for k, ref in enumerate((own_ref, p1_ref, p2_ref, p3_ref)):
        ref[...] = pieces[lax.rem(x + k, NX)]


def direct_kernel(keep_ref, recv_ref, out_ref):
    out_ref[...] = permute_lanes(keep_ref[...] + recv_ref[...], column_order(False))


def mirror_kernel(direct_ref, own_ref, q1_ref, q2_ref, q3_ref, o0_ref, o1_ref, o2_ref, o3_ref, pieces, total):
    x, y = place("occ"), place("y")
    for k, ref in enumerate((own_ref, q1_ref, q2_ref, q3_ref)):
        pieces[lax.rem(x + NX - k, NX)] = ref[...]
    left = lax.broadcasted_iota(jnp.int32, (256, 128), 1) < 64
    for t in range(2):
        even, odd = pieces[2 * t], pieces[2 * t + 1]
        lanes = pl.ds(t * 128, 128)
        total[0:256, lanes] = direct_ref[0:256, lanes] + jnp.where(left, even, pltpu.roll(odd, 64, 1))
        total[256:512, lanes] = direct_ref[256:512, lanes] + jnp.where(left, pltpu.roll(even, 64, 1), odd)
    for k, ref in enumerate((o0_ref, o1_ref, o2_ref, o3_ref)):
        ref[...] = total[pl.ds(pl.multiple_of(lax.rem(y + k, NY) * 128, 128), 128), :]


def finish_kernel(parts_ref, denom_ref, out_ref):
    n = lax.broadcasted_iota(jnp.int32, (256, 256), 1)
    g = lax.broadcasted_iota(jnp.int32, (256, 256), 0)
    back = (n == ((g // 8) % 8) * 32 + 8 * (g // 64) + g % 8).astype(F32).astype(BF16)
    acc = parts_ref[0]
    for z in range(1, NZ):
        acc = acc + parts_ref[z]
    out_ref[...] = permute_lanes(acc, back) / denom_ref[...]


def params(mib):
    return pltpu.CompilerParams(vmem_limit_bytes=mib << 20)


def f32(*shape):
    return jax.ShapeDtypeStruct(shape, F32)


def kernel_call(body, name, args, outs, scratch=()):
    single = not isinstance(outs, list)
    return pl.pallas_call(
        body,
        in_specs=[vmem_spec()] * len(args),
        out_specs=vmem_spec() if single else [vmem_spec()] * len(outs),
        out_shape=outs,
        scratch_shapes=[pltpu.VMEM(shape, F32) for shape in scratch],
        compiler_params=params(8),
        name=name,
    )(*args)


def shift_y(k):
    pairs = []
    for y in range(NY):
        to = (y + k) % NY
        for z in range(NZ):
            for core in range(2):
                core_to = core ^ (y >= 2) ^ (to >= 2)
                pairs.append(((y * NZ + z) * 2 + core, (to * NZ + z) * 2 + core_to))
    return pairs


def shift_x(k):
    return [(x, (x + k) % NX) for x in range(NX)]


def in_hbm(x):
    return pltpu.with_memory_space_constraint(x, pltpu.HBM)


def per_device(tiles, tile_slot, amplitudes, occ_energy, vir_energy):
    y, z, core, x = (place(name) for name in ("y", "z", "core", "occ"))
    keep, send = pl.pallas_call(
        ladder_kernel,
        in_specs=[pl.BlockSpec(memory_space=pltpu.HBM)] * 3,
        out_specs=[vmem_spec()] * 2,
        out_shape=[f32(512, 256)] * 2,
        scratch_shapes=[
            pltpu.SMEM((CAP,), jnp.int32),
            pltpu.VMEM((CAP, TILE, TILE), F32),
            pltpu.VMEM((COLS * TILE, 256), F32),
            pltpu.VMEM((COLS, 2 * TILE, 256), BF16),
            pltpu.VMEM((1024 + TILE, 256), F32),
            pltpu.SemaphoreType.DMA,
            pltpu.SemaphoreType.DMA((CHUNKS,)),
            pltpu.SemaphoreType.DMA((CHUNKS,)),
        ],
        compiler_params=params(24),
        name="ladder",
    )(in_hbm(tile_slot), in_hbm(tiles), in_hbm(amplitudes))
    recv = lax.ppermute(send, "core", [(0, 1), (1, 0)])
    pieces = kernel_call(
        split_kernel, "split", [keep, recv], [f32(256, 128)] * 4, [(2, 512, 128), (4, 256, 128)]
    )
    moved = [lax.ppermute(pieces[k], "occ", shift_x(k)) for k in range(1, NX)]
    direct = kernel_call(direct_kernel, "direct", [keep, recv], f32(512, 256))
    own, *others = kernel_call(
        mirror_kernel, "mirror", [direct, pieces[0], *moved], [f32(128, 256)] * 4, [(4, 256, 128), (512, 256)]
    )
    for k in range(1, NY):
        own = own + lax.ppermute(others[k - 1], VIR, shift_y(k))
    parts = lax.all_to_all(own.reshape(NZ, HALF, 256), "z", 0, 0)

    def pick(table, index):
        orbital = lax.broadcasted_iota(jnp.int32, (index.shape[0], 32), 1)
        return jnp.sum(jnp.where(index[:, None] == orbital, table[None, :], 0.0), axis=1)

    n = lax.broadcasted_iota(jnp.int32, (256,), 0)
    row = lax.broadcasted_iota(jnp.int32, (HALF,), 0)
    pair = pick(occ_energy, x * 8 + n // 32) + pick(occ_energy, n % 32)
    first = pick(vir_energy, jnp.full((HALF,), y * NZ + z, jnp.int32))
    second = pick(vir_energy, core * HALF + row)
    denominator = pair[None, :] - first[:, None] - second[:, None]
    return kernel_call(finish_kernel, "finish", [parts, denominator], f32(HALF, 256))


def solution(mesh):
    fine = Mesh(mesh.devices.reshape(NY, NZ, 2, NX), ("y", "z", "core", "occ"))
    in_specs = (P(VIR, None, None), P(VIR), P(VIR, "occ"), P(), P())
    return jax.shard_map(
        per_device, mesh=fine, in_specs=in_specs, out_specs=P(VIR, "occ"), check_vma=False
    )
```

time: 55.9 us -> 50.9 us (0.911)
  local copies, waits for them, and re-layouts: 5.04 us -> 0.01 us
  Pallas kernels: 8.78 us -> 9.35 us
    unnamed x10 -> x4, local copies, waits for them, and re-layouts: 5.04 us -> 0.01 us
    pallas_call x4 -> x5, Pallas kernels: 8.78 us -> 9.35 us  [the longest x1 7.13 us: per_device(): pl.pallas_call(ladder_kernel, in_specs=[pl.BlockSpec(memory_space=pltpu.H...]
  transfers between devices with their start and end apart: 8 -> 8, of which waited for: 7 -> 7; matrix products, arithmetic and copies ran while one was open for 1% -> 1% of each run, Pallas kernels for 0% -> 1%
where the time goes in v2:
time: 50.9 us; the launch traced here: 50.3 us
  waiting for transfers between devices  22.7 us (45%)
  starting transfers between devices  17.1 us (34%)
  Pallas kernels  9.35 us (18%)
  other arithmetic  1.04 us (2%)
    all_to_all x1, waiting for transfers between devices, per_device(): parts = lax.all_to_all(own.reshape(NZ, HALF, 256), 'z', 0, 0)  8.81 us
    all_to_all x1, starting transfers between devices, per_device(): parts = lax.all_to_all(own.reshape(NZ, HALF, 256), 'z', 0, 0)  8.32 us
    pallas_call x1, Pallas kernels, per_device(): pl.pallas_call(ladder_kernel, in_specs=[pl.BlockSpec(memory_space=pltpu.H...  7.13 us
    ppermute x3, waiting for transfers between devices, per_device(): own = own + lax.ppermute(others[k - 1], VIR, shift_y(k))  6.13 us
    ppermute x3, waiting for transfers between devices, per_device(): moved = [lax.ppermute(pieces[k], 'occ', shift_x(k)) for k in range(1, NX)]  5.89 us
    ppermute x3, starting transfers between devices, per_device(): moved = [lax.ppermute(pieces[k], 'occ', shift_x(k)) for k in range(1, NX)]  4.83 us
    ppermute x3, starting transfers between devices, per_device(): own = own + lax.ppermute(others[k - 1], VIR, shift_y(k))  3.89 us
    pallas_call x4, Pallas kernels, kernel_call(): pl.pallas_call(body, in_specs=[vmem_spec()] * len(args), out_specs=vmem_s...  2.22 us
  transfers between devices with their start and end apart: 8, of which 7 were waited for; matrix products, arithmetic and copies ran while one was open for 1% of the time, Pallas kernels for 1%

profile of v2, /device:TPU:2, one launch (start us, length us, event | category | flops | bytes accessed | tf_op | source)
XLA Modules:
  0.0 50.3 jit_solution(4185532487659493083)
XLA Ops:
  0.0 0.0 copy-start
  0.0 7.1 %ladder.1 = (f32[512,256]{1,0:T(8,128)S(1)}, f32[512,256]{1,0:T(8,128)S(1)}) custom-call(s32[64]{0:T(128)} %slot_hbm.1, f32[64,128,128]{2,1,0:T(8,128)} %tiles_hbm.1, f32[4096,256]{1,0:T(8,128)} %amps_hbm.1), custom_call_target="tpu_custom_call" | custom-call | tf_op jit(solution)/shard_map/ladder/pallas_call | solution.py:200
  7.1 0.0 copy-start.1
  7.2 0.1 collective-permute-start
  7.3 1.9 %collective-permute-done.recv_ref = f32[512,256]{1,0:T(8,128)S(1)} collective-permute-done((f32[512,256]{1,0:T(8,128)S(1)}, f32[512,256]{1,0:T(8,128)S(1)}, u32[]{:S(2)}, u32[]{:S(2)}) %collective-permute-start) | collective-permute-done | bytes 524320 | tf_op jit(solution)/shard_map/ppermute | solution.py:218
  9.2 0.7 %split.1 = (f32[256,128]{1,0:T(8,128)S(1)}, f32[256,128]{1,0:T(8,128)S(1)}, f32[256,128]{1,0:T(8,128)S(1)}, f32[256,128]{1,0:T(8,128)S(1)}) custom-call(f32[512,256]{1,0:T(8,128)S(1)} %get-tuple-element.15.keep_ref, f32[512,256]{1,0:T(8,128)S(1)} %collective-permute-done.recv_ref), custom_call_target="tpu_custom_call" | custom-call | tf_op jit(solution)/shard_map/split/pallas_call | solution.py:168
  9.9 1.6 %collective-permute-start.1 = (f32[256,128]{1,0:T(8,128)S(1)}, f32[256,128]{1,0:T(8,128)S(1)}, u32[]{:S(2)}, u32[]{:S(2)}) collective-permute-start(f32[256,128]{1,0:T(8,128)S(1)} %get-tuple-element.18), channel_id=1, source_target_pairs={{0,1},{1,2},{2,3},{3,0},{4,5},{5,6},{6,7},{7,4},{8,9},{9,10},{10,1... | collective-permute-start | bytes 393224 | tf_op jit(solution)/shard_map/ppermute | solution.py:222
  11.4 2.8 %collective-permute-start.2 = (f32[256,128]{1,0:T(8,128)S(1)}, f32[256,128]{1,0:T(8,128)S(1)}, u32[]{:S(2)}, u32[]{:S(2)}) collective-permute-start(f32[256,128]{1,0:T(8,128)S(1)} %get-tuple-element.19), channel_id=1, source_target_pairs={{0,2},{1,3},{2,0},{3,1},{4,6},{5,7},{6,4},{7,5},{8,10},{9,11},{10,... | collective-permute-start | bytes 393224 | tf_op jit(solution)/shard_map/ppermute | solution.py:222
  14.2 0.5 collective-permute-start.3
  14.7 0.4 direct.1.direct_ref
  15.1 1.4 %collective-permute-done.1.q1_ref = f32[256,128]{1,0:T(8,128)S(1)} collective-permute-done((f32[256,128]{1,0:T(8,128)S(1)}, f32[256,128]{1,0:T(8,128)S(1)}, u32[]{:S(2)}, u32[]{:S(2)}) %collective-permute-start.1) | collective-permute-done | bytes 131104 | tf_op jit(solution)/shard_map/ppermute | solution.py:222
  16.5 2.8 %collective-permute-done.2.q2_ref = f32[256,128]{1,0:T(8,128)S(1)} collective-permute-done((f32[256,128]{1,0:T(8,128)S(1)}, f32[256,128]{1,0:T(8,128)S(1)}, u32[]{:S(2)}, u32[]{:S(2)}) %collective-permute-start.2) | collective-permute-done | bytes 131104 | tf_op jit(solution)/shard_map/ppermute | solution.py:222
  19.3 1.7 %collective-permute-done.3.q3_ref = f32[256,128]{1,0:T(8,128)S(1)} collective-permute-done((f32[256,128]{1,0:T(8,128)S(1)}, f32[256,128]{1,0:T(8,128)S(1)}, u32[]{:S(2)}, u32[]{:S(2)}) %collective-permute-start.3) | collective-permute-done | bytes 131104 | tf_op jit(solution)/shard_map/ppermute | solution.py:222
  21.0 0.3 mirror.1
  21.3 1.0 %collective-permute-start.4 = (f32[128,256]{1,0:T(8,128)S(1)}, f32[128,256]{1,0:T(8,128)S(1)}, u32[]{:S(2)}, u32[]{:S(2)}) collective-permute-start(f32[128,256]{1,0:T(8,128)S(1)} %get-tuple-element.22), channel_id=1, source_target_pairs={{0,64},{4,68},{8,72},{12,76},{16,80},{20,84},{24,88},{28,92},{32,9... | collective-permute-start | bytes 393224 | tf_op jit(solution)/shard_map/ppermute | solution.py:228
  22.3 1.5 %collective-permute-start.5 = (f32[128,256]{1,0:T(8,128)S(1)}, f32[128,256]{1,0:T(8,128)S(1)}, u32[]{:S(2)}, u32[]{:S(2)}) collective-permute-start(f32[128,256]{1,0:T(8,128)S(1)} %get-tuple-element.23), channel_id=1, source_target_pairs={{0,132},{4,128},{8,140},{12,136},{16,148},{20,144},{24,156},{28,15... | collective-permute-start | bytes 393224 | tf_op jit(solution)/shard_map/ppermute | solution.py:228
  23.8 1.3 %collective-permute-start.6 = (f32[128,256]{1,0:T(8,128)S(1)}, f32[128,256]{1,0:T(8,128)S(1)}, u32[]{:S(2)}, u32[]{:S(2)}) collective-permute-start(f32[128,256]{1,0:T(8,128)S(1)} %get-tuple-element.24), channel_id=1, source_target_pairs={{0,196},{4,192},{8,204},{12,200},{16,212},{20,208},{24,220},{28,21... | collective-permute-start | bytes 393224 | tf_op jit(solution)/shard_map/ppermute | solution.py:228
  25.2 0.0 copy-done
  25.2 0.1 select_reduce_fusion
  25.3 5.9 %collective-permute-done.4 = f32[128,256]{1,0:T(8,128)S(1)} collective-permute-done((f32[128,256]{1,0:T(8,128)S(1)}, f32[128,256]{1,0:T(8,128)S(1)}, u32[]{:S(2)}, u32[]{:S(2)}) %collective-permute-start.4) | collective-permute-done | bytes 131104 | tf_op jit(solution)/shard_map/ppermute | solution.py:228
  31.1 0.0 collective-permute-done.5
  31.1 0.3 collective-permute-done.6
  31.4 0.7 %add_add_fusion = f32[128,256]{1,0:T(8,128)} fusion(f32[128,256]{1,0:T(8,128)S(1)} %collective-permute-done.6, f32[128,256]{1,0:T(8,128)S(1)} %collective-permute-done.5, f32[128,256]{1,0:T(8,128)S(1)} %get-tuple-element.21, f32[128,256]{1,0:T(8,128)S(1)} %collective-permute-done.4), kind=kLoop, calls=%fused_computation | loop fusion | flops 98304 | bytes 655360 | tf_op jit(solution)/shard_map/add | solution.py:228
  32.1 8.3 %all-to-all-start = ((f32[8,16,256]{2,1,0:T(8,128)}), f32[8,16,256]{2,1,0:T(8,128)S(1)}, u32[]{:S(2)}, u32[]{:S(2)}) async-start(f32[8,16,256]{2,1,0:T(8,128)} %bitcast), calls=%async_computation | async-start | bytes 262144 | tf_op jit(solution)/shard_map/all_to_all | solution.py:229
  40.4 0.0 copy-done.1
  40.4 0.2 select_reduce_fusion.3
  40.6 0.1 subtract_subtract_fusion.denom_ref
  40.7 8.8 %all-to-all-done.parts_ref = f32[8,16,256]{2,1,0:T(8,128)S(1)} async-done(((f32[8,16,256]{2,1,0:T(8,128)}), f32[8,16,256]{2,1,0:T(8,128)S(1)}, u32[]{:S(2)}, u32[]{:S(2)}) %all-to-all-start) | async-done | bytes 131104 | tf_op jit(solution)/shard_map/all_to_all | solution.py:229
  49.5 0.8 %finish.1 = f32[16,256]{1,0:T(8,128)} custom-call(f32[8,16,256]{2,1,0:T(8,128)S(1)} %all-to-all-done.parts_ref, f32[16,256]{1,0:T(8,128)S(1)} %subtract_subtract_fusion.denom_ref), custom_call_target="tpu_custom_call" | custom-call | tf_op jit(solution)/shard_map/finish/pallas_call | solution.py:168
  (4 shorter events, 0.0 us)
Async XLA Ops:
  0.0 25.2 %copy-start = (f32[32]{0:T(128)S(1)}, f32[32]{0:T(128)}, u32[]{:S(2)}) copy-start(f32[32]{0:T(128)} %param.8) | copy-start | bytes 388
  7.1 33.3 %copy-start.1 = (f32[32]{0:T(128)S(1)}, f32[32]{0:T(128)}, u32[]{:S(2)}) copy-start(f32[32]{0:T(128)} %param.9) | copy-start | bytes 388
  7.2 2.0 %collective-permute-start = (f32[512,256]{1,0:T(8,128)S(1)}, f32[512,256]{1,0:T(8,128)S(1)}, u32[]{:S(2)}, u32[]{:S(2)}) collective-permute-start(f32[512,256]{1,0:T(8,128)S(1)} %get-tuple-element.16), channel_id=1, source_target_pairs={{0,4},{4,0},{1,5},{5,1},{2,6},{6,2},{3,7},{7,3},{8,12},{12,8},{9,1... | collective-permute-start | bytes 1572872 | tf_op jit(solution)/shard_map/ppermute | solution.py:218
  9.9 6.7 %collective-permute-start.1 = (f32[256,128]{1,0:T(8,128)S(1)}, f32[256,128]{1,0:T(8,128)S(1)}, u32[]{:S(2)}, u32[]{:S(2)}) collective-permute-start(f32[256,128]{1,0:T(8,128)S(1)} %get-tuple-element.18), channel_id=1, source_target_pairs={{0,1},{1,2},{2,3},{3,0},{4,5},{5,6},{6,7},{7,4},{8,9},{9,10},{10,1... | collective-permute-start | bytes 393224 | tf_op jit(solution)/shard_map/ppermute | solution.py:222
  11.4 7.9 %collective-permute-start.2 = (f32[256,128]{1,0:T(8,128)S(1)}, f32[256,128]{1,0:T(8,128)S(1)}, u32[]{:S(2)}, u32[]{:S(2)}) collective-permute-start(f32[256,128]{1,0:T(8,128)S(1)} %get-tuple-element.19), channel_id=1, source_target_pairs={{0,2},{1,3},{2,0},{3,1},{4,6},{5,7},{6,4},{7,5},{8,10},{9,11},{10,... | collective-permute-start | bytes 393224 | tf_op jit(solution)/shard_map/ppermute | solution.py:222
  14.2 6.8 %collective-permute-start.3 = (f32[256,128]{1,0:T(8,128)S(1)}, f32[256,128]{1,0:T(8,128)S(1)}, u32[]{:S(2)}, u32[]{:S(2)}) collective-permute-start(f32[256,128]{1,0:T(8,128)S(1)} %get-tuple-element.20), channel_id=1, source_target_pairs={{0,3},{1,0},{2,1},{3,2},{4,7},{5,4},{6,5},{7,6},{8,11},{9,8},{10,9... | collective-permute-start | bytes 393224 | tf_op jit(solution)/shard_map/ppermute | solution.py:222
  21.3 9.8 %collective-permute-start.4 = (f32[128,256]{1,0:T(8,128)S(1)}, f32[128,256]{1,0:T(8,128)S(1)}, u32[]{:S(2)}, u32[]{:S(2)}) collective-permute-start(f32[128,256]{1,0:T(8,128)S(1)} %get-tuple-element.22), channel_id=1, source_target_pairs={{0,64},{4,68},{8,72},{12,76},{16,80},{20,84},{24,88},{28,92},{32,9... | collective-permute-start | bytes 393224 | tf_op jit(solution)/shard_map/ppermute | solution.py:228
  22.3 8.8 %collective-permute-start.5 = (f32[128,256]{1,0:T(8,128)S(1)}, f32[128,256]{1,0:T(8,128)S(1)}, u32[]{:S(2)}, u32[]{:S(2)}) collective-permute-start(f32[128,256]{1,0:T(8,128)S(1)} %get-tuple-element.23), channel_id=1, source_target_pairs={{0,132},{4,128},{8,140},{12,136},{16,148},{20,144},{24,156},{28,15... | collective-permute-start | bytes 393224 | tf_op jit(solution)/shard_map/ppermute | solution.py:228
  23.8 7.6 %collective-permute-start.6 = (f32[128,256]{1,0:T(8,128)S(1)}, f32[128,256]{1,0:T(8,128)S(1)}, u32[]{:S(2)}, u32[]{:S(2)}) collective-permute-start(f32[128,256]{1,0:T(8,128)S(1)} %get-tuple-element.24), channel_id=1, source_target_pairs={{0,196},{4,192},{8,204},{12,200},{16,212},{20,208},{24,220},{28,21... | collective-permute-start | bytes 393224 | tf_op jit(solution)/shard_map/ppermute | solution.py:228
  32.1 17.4 %all-to-all-start = ((f32[8,16,256]{2,1,0:T(8,128)}), f32[8,16,256]{2,1,0:T(8,128)S(1)}, u32[]{:S(2)}, u32[]{:S(2)}) async-start(f32[8,16,256]{2,1,0:T(8,128)} %bitcast), calls=%async_computation | async-start | bytes 262144 | tf_op jit(solution)/shard_map/all_to_all | solution.py:229

commit v3 on v2

--- a/solution.py
+++ b/solution.py
@@ -18,6 +18,7 @@
 HALF = 16
 EIGHT = 8
 VIR = ("y", "z", "core")
+Z_ORDER = (4, 5, 6, 7, 0, 1, 2, 3)
 
 
 def vmem_spec():
@@ -45,6 +46,10 @@
 
 def place(name):
     return lax.axis_index(name).astype(jnp.int32)
+
+
+def turn(position, k, size, which):
+    return lax.rem(position + size + k * (1 - 2 * which), size)
 
 
 def ladder_kernel(slot_hbm, tiles_hbm, amps_hbm, *rest):
@@ -124,7 +129,7 @@
             pieces[2 * t, rows, :] = jnp.where(left, one, pltpu.roll(two, 64, 1))
             pieces[2 * t + 1, rows, :] = jnp.where(left, pltpu.roll(one, 64, 1), two)
     for k, ref in enumerate((own_ref, p1_ref, p2_ref, p3_ref)):
-        ref[...] = pieces[lax.rem(x + k, NX)]
+        ref[...] = pieces[turn(x, k, NX, place("core"))]
 
 
 def direct_kernel(keep_ref, recv_ref, out_ref):
@@ -132,9 +137,9 @@
 
 
 def mirror_kernel(direct_ref, own_ref, q1_ref, q2_ref, q3_ref, o0_ref, o1_ref, o2_ref, o3_ref, pieces, total):
-    x, y = place("occ"), place("y")
+    x, y, core = place("occ"), place("y"), place("core")
     for k, ref in enumerate((own_ref, q1_ref, q2_ref, q3_ref)):
-        pieces[lax.rem(x + NX - k, NX)] = ref[...]
+        pieces[turn(x, -k, NX, core)] = ref[...]
     left = lax.broadcasted_iota(jnp.int32, (256, 128), 1) < 64
     for t in range(2):
         even, odd = pieces[2 * t], pieces[2 * t + 1]
@@ -142,7 +147,13 @@
         total[0:256, lanes] = direct_ref[0:256, lanes] + jnp.where(left, even, pltpu.roll(odd, 64, 1))
         total[256:512, lanes] = direct_ref[256:512, lanes] + jnp.where(left, pltpu.roll(even, 64, 1), odd)
     for k, ref in enumerate((o0_ref, o1_ref, o2_ref, o3_ref)):
-        ref[...] = total[pl.ds(pl.multiple_of(lax.rem(y + k, NY) * 128, 128), 128), :]
+        ref[...] = total[pl.ds(pl.multiple_of(turn(y, k, NY, row_set(y, core)) * 128, 128), 128), :]
+
+
+def gather_kernel(r0_ref, r1_ref, r2_ref, r3_ref, out_ref):
+    for p, z in enumerate(Z_ORDER):
+        rows = pl.ds(z * HALF, HALF)
+        out_ref[p] = (r0_ref[rows, :] + r1_ref[rows, :]) + (r2_ref[rows, :] + r3_ref[rows, :])
 
 
 def finish_kernel(parts_ref, denom_ref, out_ref):
@@ -179,16 +190,23 @@
 def shift_y(k):
     pairs = []
     for y in range(NY):
-        to = (y + k) % NY
         for z in range(NZ):
             for core in range(2):
-                core_to = core ^ (y >= 2) ^ (to >= 2)
+                s = core ^ (y >= NY // 2)
+                to = (y + (k if s == 0 else -k)) % NY
+                core_to = s ^ (to >= NY // 2)
                 pairs.append(((y * NZ + z) * 2 + core, (to * NZ + z) * 2 + core_to))
     return pairs
 
 
 def shift_x(k):
-    return [(x, (x + k) % NX) for x in range(NX)]
+    return [
+        (core * NX + x, core * NX + (x + (k if core == 0 else -k)) % NX) for core in range(2) for x in range(NX)
+    ]
+
+
+def z_groups():
+    return [[(y * NZ + z) * 2 + core for z in Z_ORDER] for y in range(NY) for core in range(2)]
 
 
 def in_hbm(x):
@@ -219,14 +237,14 @@
     pieces = kernel_call(
         split_kernel, "split", [keep, recv], [f32(256, 128)] * 4, [(2, 512, 128), (4, 256, 128)]
     )
-    moved = [lax.ppermute(pieces[k], "occ", shift_x(k)) for k in range(1, NX)]
+    moved = [lax.ppermute(pieces[k], ("core", "occ"), shift_x(k)) for k in range(1, NX)]
     direct = kernel_call(direct_kernel, "direct", [keep, recv], f32(512, 256))
     own, *others = kernel_call(
         mirror_kernel, "mirror", [direct, pieces[0], *moved], [f32(128, 256)] * 4, [(4, 256, 128), (512, 256)]
     )
-    for k in range(1, NY):
-        own = own + lax.ppermute(others[k - 1], VIR, shift_y(k))
-    parts = lax.all_to_all(own.reshape(NZ, HALF, 256), "z", 0, 0)
+    moved = [lax.ppermute(others[k - 1], VIR, shift_y(k)) for k in range(1, NY)]
+    summed = kernel_call(gather_kernel, "gather", [own, *moved], f32(NZ, HALF, 256))
+    parts = lax.all_to_all(summed, VIR, 0, 0, axis_index_groups=z_groups())
 
     def pick(table, index):
         orbital = lax.broadcasted_iota(jnp.int32, (index.shape[0], 32), 1)

time: 50.9 us -> 48.8 us (0.959)
  the two profiles are of different devices: /device:TPU:2 before, /device:TPU:1 now
where the time goes in v3:
time: 48.8 us; the launch traced here: 48.6 us
  waiting for transfers between devices  19.7 us (40%)
  starting transfers between devices  18.5 us (38%)
  Pallas kernels  10 us (20%)
    all_to_all x1, starting transfers between devices, per_device(): parts = lax.all_to_all(summed, VIR, 0, 0, axis_index_groups=z_groups())  10.2 us
    ppermute x3, waiting for transfers between devices, per_device(): lax.ppermute(pieces[k], ('core', 'occ'), shift_x(k))  7.76 us
    pallas_call x1, Pallas kernels, per_device(): pl.pallas_call(ladder_kernel, in_specs=[pl.BlockSpec(memory_space=pltpu.H...  7.12 us
    ppermute x3, waiting for transfers between devices, per_device(): moved = [lax.ppermute(others[k - 1], VIR, shift_y(k)) for k in range(1, NY)]  6.37 us
    all_to_all x1, waiting for transfers between devices, per_device(): parts = lax.all_to_all(summed, VIR, 0, 0, axis_index_groups=z_groups())  4.02 us
    ppermute x1, starting transfers between devices, per_device(): recv = lax.ppermute(send, 'core', [(0, 1), (1, 0)])  3.29 us
    ppermute x3, starting transfers between devices, per_device(): moved = [lax.ppermute(others[k - 1], VIR, shift_y(k)) for k in range(1, NY)]  3.08 us
    pallas_call x5, Pallas kernels, kernel_call(): pl.pallas_call(body, in_specs=[vmem_spec()] * len(args), out_specs=vmem_s...  2.89 us
  transfers between devices with their start and end apart: 8, of which 8 were waited for; matrix products, arithmetic and copies ran while one was open for 1% of the time, Pallas kernels for 1%

profile of v3, /device:TPU:1, one launch (start us, length us, event | category | flops | bytes accessed | tf_op | source)
XLA Modules:
  0.0 48.6 jit_solution(5035310748441410747)
XLA Ops:
  0.0 0.0 copy-start
  0.0 7.1 %ladder.1 = (f32[512,256]{1,0:T(8,128)S(1)}, f32[512,256]{1,0:T(8,128)S(1)}) custom-call(s32[64]{0:T(128)} %slot_hbm.1, f32[64,128,128]{2,1,0:T(8,128)} %tiles_hbm.1, f32[4096,256]{1,0:T(8,128)} %amps_hbm.1), custom_call_target="tpu_custom_call" | custom-call | tf_op jit(solution)/shard_map/ladder/pallas_call | solution.py:218
  7.1 0.0 copy-start.1
  7.1 3.3 %collective-permute-start = (f32[512,256]{1,0:T(8,128)S(1)}, f32[512,256]{1,0:T(8,128)S(1)}, u32[]{:S(2)}, u32[]{:S(2)}) collective-permute-start(f32[512,256]{1,0:T(8,128)S(1)} %get-tuple-element.16), channel_id=1, source_target_pairs={{0,4},{4,0},{1,5},{5,1},{2,6},{6,2},{3,7},{7,3},{8,12},{12,8},{9,1... | collective-permute-start | bytes 1572872 | tf_op jit(solution)/shard_map/ppermute | solution.py:236
  10.4 1.5 %collective-permute-done.recv_ref = f32[512,256]{1,0:T(8,128)S(1)} collective-permute-done((f32[512,256]{1,0:T(8,128)S(1)}, f32[512,256]{1,0:T(8,128)S(1)}, u32[]{:S(2)}, u32[]{:S(2)}) %collective-permute-start) | collective-permute-done | bytes 524320 | tf_op jit(solution)/shard_map/ppermute | solution.py:236
  12.0 0.7 %split.1 = (f32[256,128]{1,0:T(8,128)S(1)}, f32[256,128]{1,0:T(8,128)S(1)}, f32[256,128]{1,0:T(8,128)S(1)}, f32[256,128]{1,0:T(8,128)S(1)}) custom-call(f32[512,256]{1,0:T(8,128)S(1)} %get-tuple-element.15.keep_ref, f32[512,256]{1,0:T(8,128)S(1)} %collective-permute-done.recv_ref), custom_call_target="tpu_custom_call" | custom-call | tf_op jit(solution)/shard_map/split/pallas_call | solution.py:179
  12.7 0.9 %collective-permute-start.1 = (f32[256,128]{1,0:T(8,128)S(1)}, f32[256,128]{1,0:T(8,128)S(1)}, u32[]{:S(2)}, u32[]{:S(2)}) collective-permute-start(f32[256,128]{1,0:T(8,128)S(1)} %get-tuple-element.18), channel_id=1, source_target_pairs={{0,1},{1,2},{2,3},{3,0},{4,7},{5,4},{6,5},{7,6},{8,9},{9,10},{10,1... | collective-permute-start | bytes 393224 | tf_op jit(solution)/shard_map/ppermute | solution.py:240
  13.5 0.5 %collective-permute-start.2 = (f32[256,128]{1,0:T(8,128)S(1)}, f32[256,128]{1,0:T(8,128)S(1)}, u32[]{:S(2)}, u32[]{:S(2)}) collective-permute-start(f32[256,128]{1,0:T(8,128)S(1)} %get-tuple-element.19), channel_id=1, source_target_pairs={{0,2},{1,3},{2,0},{3,1},{4,6},{5,7},{6,4},{7,5},{8,10},{9,11},{10,... | collective-permute-start | bytes 393224 | tf_op jit(solution)/shard_map/ppermute | solution.py:240
  14.1 0.6 %collective-permute-start.3 = (f32[256,128]{1,0:T(8,128)S(1)}, f32[256,128]{1,0:T(8,128)S(1)}, u32[]{:S(2)}, u32[]{:S(2)}) collective-permute-start(f32[256,128]{1,0:T(8,128)S(1)} %get-tuple-element.20), channel_id=1, source_target_pairs={{0,3},{1,0},{2,1},{3,2},{4,5},{5,6},{6,7},{7,4},{8,11},{9,8},{10,9... | collective-permute-start | bytes 393224 | tf_op jit(solution)/shard_map/ppermute | solution.py:240
  14.7 0.4 direct.1.direct_ref
  15.1 1.5 %collective-permute-done.1.q1_ref = f32[256,128]{1,0:T(8,128)S(1)} collective-permute-done((f32[256,128]{1,0:T(8,128)S(1)}, f32[256,128]{1,0:T(8,128)S(1)}, u32[]{:S(2)}, u32[]{:S(2)}) %collective-permute-start.1) | collective-permute-done | bytes 131104 | tf_op jit(solution)/shard_map/ppermute | solution.py:240
  16.6 4.0 %collective-permute-done.2.q2_ref = f32[256,128]{1,0:T(8,128)S(1)} collective-permute-done((f32[256,128]{1,0:T(8,128)S(1)}, f32[256,128]{1,0:T(8,128)S(1)}, u32[]{:S(2)}, u32[]{:S(2)}) %collective-permute-start.2) | collective-permute-done | bytes 131104 | tf_op jit(solution)/shard_map/ppermute | solution.py:240
  20.6 2.2 %collective-permute-done.3.q3_ref = f32[256,128]{1,0:T(8,128)S(1)} collective-permute-done((f32[256,128]{1,0:T(8,128)S(1)}, f32[256,128]{1,0:T(8,128)S(1)}, u32[]{:S(2)}, u32[]{:S(2)}) %collective-permute-start.3) | collective-permute-done | bytes 131104 | tf_op jit(solution)/shard_map/ppermute | solution.py:240
  22.8 0.3 mirror.1
  23.1 1.8 %collective-permute-start.4 = (f32[128,256]{1,0:T(8,128)S(1)}, f32[128,256]{1,0:T(8,128)S(1)}, u32[]{:S(2)}, u32[]{:S(2)}) collective-permute-start(f32[128,256]{1,0:T(8,128)S(1)} %get-tuple-element.22), channel_id=1, source_target_pairs={{0,64},{4,192},{8,72},{12,200},{16,80},{20,208},{24,88},{28,216},{... | collective-permute-start | bytes 393224 | tf_op jit(solution)/shard_map/ppermute | solution.py:245
  24.9 0.6 %collective-permute-start.5 = (f32[128,256]{1,0:T(8,128)S(1)}, f32[128,256]{1,0:T(8,128)S(1)}, u32[]{:S(2)}, u32[]{:S(2)}) collective-permute-start(f32[128,256]{1,0:T(8,128)S(1)} %get-tuple-element.23), channel_id=1, source_target_pairs={{0,132},{4,128},{8,140},{12,136},{16,148},{20,144},{24,156},{28,15... | collective-permute-start | bytes 393224 | tf_op jit(solution)/shard_map/ppermute | solution.py:245
  25.5 0.7 %collective-permute-start.6 = (f32[128,256]{1,0:T(8,128)S(1)}, f32[128,256]{1,0:T(8,128)S(1)}, u32[]{:S(2)}, u32[]{:S(2)}) collective-permute-start(f32[128,256]{1,0:T(8,128)S(1)} %get-tuple-element.24), channel_id=1, source_target_pairs={{0,196},{4,68},{8,204},{12,76},{16,212},{20,84},{24,220},{28,92},{... | collective-permute-start | bytes 393224 | tf_op jit(solution)/shard_map/ppermute | solution.py:245
  26.2 0.0 copy-done
  26.2 0.1 select_reduce_fusion
  26.3 3.4 %collective-permute-done.4.r1_ref = f32[128,256]{1,0:T(8,128)S(1)} collective-permute-done((f32[128,256]{1,0:T(8,128)S(1)}, f32[128,256]{1,0:T(8,128)S(1)}, u32[]{:S(2)}, u32[]{:S(2)}) %collective-permute-start.4) | collective-permute-done | bytes 131104 | tf_op jit(solution)/shard_map/ppermute | solution.py:245
  29.7 1.6 %collective-permute-done.5.r2_ref = f32[128,256]{1,0:T(8,128)S(1)} collective-permute-done((f32[128,256]{1,0:T(8,128)S(1)}, f32[128,256]{1,0:T(8,128)S(1)}, u32[]{:S(2)}, u32[]{:S(2)}) %collective-permute-start.5) | collective-permute-done | bytes 131104 | tf_op jit(solution)/shard_map/ppermute | solution.py:245
  31.3 1.3 %collective-permute-done.6.r3_ref = f32[128,256]{1,0:T(8,128)S(1)} collective-permute-done((f32[128,256]{1,0:T(8,128)S(1)}, f32[128,256]{1,0:T(8,128)S(1)}, u32[]{:S(2)}, u32[]{:S(2)}) %collective-permute-start.6) | collective-permute-done | bytes 131104 | tf_op jit(solution)/shard_map/ppermute | solution.py:245
  32.7 0.7 %gather.1 = f32[8,16,256]{2,1,0:T(8,128)} custom-call(f32[128,256]{1,0:T(8,128)S(1)} %get-tuple-element.21.r0_ref, f32[128,256]{1,0:T(8,128)S(1)} %collective-permute-done.4.r1_ref, f32[128,256]{1,0:T(8,128)S(1)} %collective-permute-done.5.r2_ref, f32[128,256]{1,0:T(8,128)S(1)} %collective-permute-done.6.r3_ref), custom_call_target="tpu_custom_call" | custom-call | tf_op jit(solution)/shard_map/gather/pallas_call | solution.py:179
  33.3 10.2 %all-to-all-start = ((f32[8,16,256]{2,1,0:T(8,128)}), f32[8,16,256]{2,1,0:T(8,128)S(1)}, u32[]{:S(2)}, u32[]{:S(2)}) async-start(f32[8,16,256]{2,1,0:T(8,128)} %gather.1), calls=%async_computation | async-start | bytes 262144 | tf_op jit(solution)/shard_map/all_to_all | solution.py:247
  43.5 0.0 copy-done.1
  43.5 0.2 select_reduce_fusion.3
  43.7 0.1 subtract_subtract_fusion.denom_ref
  43.8 4.0 %all-to-all-done.parts_ref = f32[8,16,256]{2,1,0:T(8,128)S(1)} async-done(((f32[8,16,256]{2,1,0:T(8,128)}), f32[8,16,256]{2,1,0:T(8,128)S(1)}, u32[]{:S(2)}, u32[]{:S(2)}) %all-to-all-start) | async-done | bytes 131104 | tf_op jit(solution)/shard_map/all_to_all | solution.py:247
  47.8 0.8 %finish.1 = f32[16,256]{1,0:T(8,128)} custom-call(f32[8,16,256]{2,1,0:T(8,128)S(1)} %all-to-all-done.parts_ref, f32[16,256]{1,0:T(8,128)S(1)} %subtract_subtract_fusion.denom_ref), custom_call_target="tpu_custom_call" | custom-call | tf_op jit(solution)/shard_map/finish/pallas_call | solution.py:179
  (4 shorter events, 0.0 us)
Async XLA Ops:
  0.0 26.2 %copy-start = (f32[32]{0:T(128)S(1)}, f32[32]{0:T(128)}, u32[]{:S(2)}) copy-start(f32[32]{0:T(128)} %param.8) | copy-start | bytes 388
  7.1 36.4 %copy-start.1 = (f32[32]{0:T(128)S(1)}, f32[32]{0:T(128)}, u32[]{:S(2)}) copy-start(f32[32]{0:T(128)} %param.9) | copy-start | bytes 388
  7.1 4.8 %collective-permute-start = (f32[512,256]{1,0:T(8,128)S(1)}, f32[512,256]{1,0:T(8,128)S(1)}, u32[]{:S(2)}, u32[]{:S(2)}) collective-permute-start(f32[512,256]{1,0:T(8,128)S(1)} %get-tuple-element.16), channel_id=1, source_target_pairs={{0,4},{4,0},{1,5},{5,1},{2,6},{6,2},{3,7},{7,3},{8,12},{12,8},{9,1... | collective-permute-start | bytes 1572872 | tf_op jit(solution)/shard_map/ppermute | solution.py:236
  12.7 3.9 %collective-permute-start.1 = (f32[256,128]{1,0:T(8,128)S(1)}, f32[256,128]{1,0:T(8,128)S(1)}, u32[]{:S(2)}, u32[]{:S(2)}) collective-permute-start(f32[256,128]{1,0:T(8,128)S(1)} %get-tuple-element.18), channel_id=1, source_target_pairs={{0,1},{1,2},{2,3},{3,0},{4,7},{5,4},{6,5},{7,6},{8,9},{9,10},{10,1... | collective-permute-start | bytes 393224 | tf_op jit(solution)/shard_map/ppermute | solution.py:240
  13.5 7.1 %collective-permute-start.2 = (f32[256,128]{1,0:T(8,128)S(1)}, f32[256,128]{1,0:T(8,128)S(1)}, u32[]{:S(2)}, u32[]{:S(2)}) collective-permute-start(f32[256,128]{1,0:T(8,128)S(1)} %get-tuple-element.19), channel_id=1, source_target_pairs={{0,2},{1,3},{2,0},{3,1},{4,6},{5,7},{6,4},{7,5},{8,10},{9,11},{10,... | collective-permute-start | bytes 393224 | tf_op jit(solution)/shard_map/ppermute | solution.py:240
  14.1 8.8 %collective-permute-start.3 = (f32[256,128]{1,0:T(8,128)S(1)}, f32[256,128]{1,0:T(8,128)S(1)}, u32[]{:S(2)}, u32[]{:S(2)}) collective-permute-start(f32[256,128]{1,0:T(8,128)S(1)} %get-tuple-element.20), channel_id=1, source_target_pairs={{0,3},{1,0},{2,1},{3,2},{4,5},{5,6},{6,7},{7,4},{8,11},{9,8},{10,9... | collective-permute-start | bytes 393224 | tf_op jit(solution)/shard_map/ppermute | solution.py:240
  23.1 6.6 %collective-permute-start.4 = (f32[128,256]{1,0:T(8,128)S(1)}, f32[128,256]{1,0:T(8,128)S(1)}, u32[]{:S(2)}, u32[]{:S(2)}) collective-permute-start(f32[128,256]{1,0:T(8,128)S(1)} %get-tuple-element.22), channel_id=1, source_target_pairs={{0,64},{4,192},{8,72},{12,200},{16,80},{20,208},{24,88},{28,216},{... | collective-permute-start | bytes 393224 | tf_op jit(solution)/shard_map/ppermute | solution.py:245
  24.9 6.5 %collective-permute-start.5 = (f32[128,256]{1,0:T(8,128)S(1)}, f32[128,256]{1,0:T(8,128)S(1)}, u32[]{:S(2)}, u32[]{:S(2)}) collective-permute-start(f32[128,256]{1,0:T(8,128)S(1)} %get-tuple-element.23), channel_id=1, source_target_pairs={{0,132},{4,128},{8,140},{12,136},{16,148},{20,144},{24,156},{28,15... | collective-permute-start | bytes 393224 | tf_op jit(solution)/shard_map/ppermute | solution.py:245
  25.5 7.2 %collective-permute-start.6 = (f32[128,256]{1,0:T(8,128)S(1)}, f32[128,256]{1,0:T(8,128)S(1)}, u32[]{:S(2)}, u32[]{:S(2)}) collective-permute-start(f32[128,256]{1,0:T(8,128)S(1)} %get-tuple-element.24), channel_id=1, source_target_pairs={{0,196},{4,68},{8,204},{12,76},{16,212},{20,84},{24,220},{28,92},{... | collective-permute-start | bytes 393224 | tf_op jit(solution)/shard_map/ppermute | solution.py:245
  33.3 14.5 %all-to-all-start = ((f32[8,16,256]{2,1,0:T(8,128)}), f32[8,16,256]{2,1,0:T(8,128)S(1)}, u32[]{:S(2)}, u32[]{:S(2)}) async-start(f32[8,16,256]{2,1,0:T(8,128)} %gather.1), calls=%async_computation | async-start | bytes 262144 | tf_op jit(solution)/shard_map/all_to_all | solution.py:247

commit v4 on v3

--- a/solution.py
+++ b/solution.py
@@ -13,8 +13,9 @@
 TILE = 128
 CAP = 64
 COLS = 32
-CHUNKS = 8
+CHUNKS = 4
 NY, NZ, NX = 4, 8, 4
+STEPS = (0, 2, 1, 3)
 HALF = 16
 EIGHT = 8
 VIR = ("y", "z", "core")
@@ -68,13 +69,12 @@
     slot_copy.start()
     for c in range(CHUNKS):
         amp_copy(c).start()
-    for c in range(CHUNKS):
-        tile_copy(c).start()
     acc[...] = jnp.zeros_like(acc)
 
     @pl.loop(0, CHUNKS)
     def _(c):
         amp_copy(c).wait()
+        tile_copy(c).start()
         for q in range(arows // TILE):
             block = c * (arows // TILE) + q
             a = abuf[pl.ds(pl.multiple_of(block * TILE, TILE), TILE), :]
@@ -128,7 +128,7 @@
             two = xbuf[t, pl.ds((1 - s) * 256 + a, HALF, stride=HALF), :]
             pieces[2 * t, rows, :] = jnp.where(left, one, pltpu.roll(two, 64, 1))
             pieces[2 * t + 1, rows, :] = jnp.where(left, pltpu.roll(one, 64, 1), two)
-    for k, ref in enumerate((own_ref, p1_ref, p2_ref, p3_ref)):
+    for k, ref in zip(STEPS, (own_ref, p1_ref, p2_ref, p3_ref)):
         ref[...] = pieces[turn(x, k, NX, place("core"))]
 
 
@@ -138,7 +138,7 @@
 
 def mirror_kernel(direct_ref, own_ref, q1_ref, q2_ref, q3_ref, o0_ref, o1_ref, o2_ref, o3_ref, pieces, total):
     x, y, core = place("occ"), place("y"), place("core")
-    for k, ref in enumerate((own_ref, q1_ref, q2_ref, q3_ref)):
+    for k, ref in zip(STEPS, (own_ref, q1_ref, q2_ref, q3_ref)):
         pieces[turn(x, -k, NX, core)] = ref[...]
     left = lax.broadcasted_iota(jnp.int32, (256, 128), 1) < 64
     for t in range(2):
@@ -146,7 +146,7 @@
         lanes = pl.ds(t * 128, 128)
         total[0:256, lanes] = direct_ref[0:256, lanes] + jnp.where(left, even, pltpu.roll(odd, 64, 1))
         total[256:512, lanes] = direct_ref[256:512, lanes] + jnp.where(left, pltpu.roll(even, 64, 1), odd)
-    for k, ref in enumerate((o0_ref, o1_ref, o2_ref, o3_ref)):
+    for k, ref in zip(STEPS, (o0_ref, o1_ref, o2_ref, o3_ref)):
         ref[...] = total[pl.ds(pl.multiple_of(turn(y, k, NY, row_set(y, core)) * 128, 128), 128), :]
 
 
@@ -237,12 +237,12 @@
     pieces = kernel_call(
         split_kernel, "split", [keep, recv], [f32(256, 128)] * 4, [(2, 512, 128), (4, 256, 128)]
     )
-    moved = [lax.ppermute(pieces[k], ("core", "occ"), shift_x(k)) for k in range(1, NX)]
+    moved = [lax.ppermute(pieces[n], ("core", "occ"), shift_x(STEPS[n])) for n in range(1, NX)]
     direct = kernel_call(direct_kernel, "direct", [keep, recv], f32(512, 256))
     own, *others = kernel_call(
         mirror_kernel, "mirror", [direct, pieces[0], *moved], [f32(128, 256)] * 4, [(4, 256, 128), (512, 256)]
     )
-    moved = [lax.ppermute(others[k - 1], VIR, shift_y(k)) for k in range(1, NY)]
+    moved = [lax.ppermute(others[n - 1], VIR, shift_y(STEPS[n])) for n in range(1, NY)]
     summed = kernel_call(gather_kernel, "gather", [own, *moved], f32(NZ, HALF, 256))
     parts = lax.all_to_all(summed, VIR, 0, 0, axis_index_groups=z_groups())
 

time: 48.8 us -> 46.5 us (0.953)
  waiting for transfers between devices: 19.7 us -> 18.1 us
  Pallas kernels: 10 us -> 8.63 us
  starting transfers between devices: 18.5 us -> 19.2 us
    pallas_call x1, Pallas kernels: 7.12 us -> 5.75 us  [per_device(): pl.pallas_call(ladder_kernel, in_specs=[pl.BlockSpec(memory_space=pltpu.H...]
    ppermute x6, starting transfers between devices: 5.06 us -> 6.33 us  [the longest x3 3.74 us: per_device(): lax.ppermute(others[n - 1], VIR, shift_y(STEPS[n]))]
    ppermute x6, waiting for transfers between devices: 14.1 us -> 13.1 us  [the longest x3 6.89 us: per_device(): lax.ppermute(pieces[n], ('core', 'occ'), shift_x(STEPS[n]))]
    all_to_all x1, starting transfers between devices: 10.2 us -> 9.54 us  [per_device(): parts = lax.all_to_all(summed, VIR, 0, 0, axis_index_groups=z_groups())]
    all_to_all x1, waiting for transfers between devices: 4.02 us -> 3.43 us  [per_device(): parts = lax.all_to_all(summed, VIR, 0, 0, axis_index_groups=z_groups())]
where the time goes in v4:
time: 46.5 us; the launch traced here: 46.3 us
  starting transfers between devices  19.2 us (41%)
  waiting for transfers between devices  18.1 us (39%)
  Pallas kernels  8.63 us (19%)
    all_to_all x1, starting transfers between devices, per_device(): parts = lax.all_to_all(summed, VIR, 0, 0, axis_index_groups=z_groups())  9.54 us
    ppermute x3, waiting for transfers between devices, per_device(): lax.ppermute(pieces[n], ('core', 'occ'), shift_x(STEPS[n]))  6.89 us
    ppermute x3, waiting for transfers between devices, per_device(): lax.ppermute(others[n - 1], VIR, shift_y(STEPS[n]))  6.26 us
    pallas_call x1, Pallas kernels, per_device(): pl.pallas_call(ladder_kernel, in_specs=[pl.BlockSpec(memory_space=pltpu.H...  5.75 us
    ppermute x3, starting transfers between devices, per_device(): lax.ppermute(others[n - 1], VIR, shift_y(STEPS[n]))  3.74 us
    all_to_all x1, waiting for transfers between devices, per_device(): parts = lax.all_to_all(summed, VIR, 0, 0, axis_index_groups=z_groups())  3.43 us
    ppermute x1, starting transfers between devices, per_device(): recv = lax.ppermute(send, 'core', [(0, 1), (1, 0)])  3.29 us
    pallas_call x5, Pallas kernels, kernel_call(): pl.pallas_call(body, in_specs=[vmem_spec()] * len(args), out_specs=vmem_s...  2.88 us
  transfers between devices with their start and end apart: 8, of which 8 were waited for; matrix products, arithmetic and copies ran while one was open for 1% of the time, Pallas kernels for 1%

profile of v4, /device:TPU:1, one launch (start us, length us, event | category | flops | bytes accessed | tf_op | source)
XLA Modules:
  0.0 46.3 jit_solution(14526365744425779211)
XLA Ops:
  0.0 0.0 copy-start
  0.0 5.8 %ladder.1 = (f32[512,256]{1,0:T(8,128)S(1)}, f32[512,256]{1,0:T(8,128)S(1)}) custom-call(s32[64]{0:T(128)} %slot_hbm.1, f32[64,128,128]{2,1,0:T(8,128)} %tiles_hbm.1, f32[4096,256]{1,0:T(8,128)} %amps_hbm.1), custom_call_target="tpu_custom_call" | custom-call | tf_op jit(solution)/shard_map/ladder/pallas_call | solution.py:218
  5.8 0.0 copy-start.1
  5.8 3.3 %collective-permute-start = (f32[512,256]{1,0:T(8,128)S(1)}, f32[512,256]{1,0:T(8,128)S(1)}, u32[]{:S(2)}, u32[]{:S(2)}) collective-permute-start(f32[512,256]{1,0:T(8,128)S(1)} %get-tuple-element.16), channel_id=1, source_target_pairs={{0,4},{4,0},{1,5},{5,1},{2,6},{6,2},{3,7},{7,3},{8,12},{12,8},{9,1... | collective-permute-start | bytes 1572872 | tf_op jit(solution)/shard_map/ppermute | solution.py:236
  9.1 1.5 %collective-permute-done.recv_ref = f32[512,256]{1,0:T(8,128)S(1)} collective-permute-done((f32[512,256]{1,0:T(8,128)S(1)}, f32[512,256]{1,0:T(8,128)S(1)}, u32[]{:S(2)}, u32[]{:S(2)}) %collective-permute-start) | collective-permute-done | bytes 524320 | tf_op jit(solution)/shard_map/ppermute | solution.py:236
  10.6 0.7 %split.1 = (f32[256,128]{1,0:T(8,128)S(1)}, f32[256,128]{1,0:T(8,128)S(1)}, f32[256,128]{1,0:T(8,128)S(1)}, f32[256,128]{1,0:T(8,128)S(1)}) custom-call(f32[512,256]{1,0:T(8,128)S(1)} %get-tuple-element.15.keep_ref, f32[512,256]{1,0:T(8,128)S(1)} %collective-permute-done.recv_ref), custom_call_target="tpu_custom_call" | custom-call | tf_op jit(solution)/shard_map/split/pallas_call | solution.py:179
  11.3 1.1 %collective-permute-start.1 = (f32[256,128]{1,0:T(8,128)S(1)}, f32[256,128]{1,0:T(8,128)S(1)}, u32[]{:S(2)}, u32[]{:S(2)}) collective-permute-start(f32[256,128]{1,0:T(8,128)S(1)} %get-tuple-element.18), channel_id=1, source_target_pairs={{0,2},{1,3},{2,0},{3,1},{4,6},{5,7},{6,4},{7,5},{8,10},{9,11},{10,... | collective-permute-start | bytes 393224 | tf_op jit(solution)/shard_map/ppermute | solution.py:240
  12.4 0.9 %collective-permute-start.2 = (f32[256,128]{1,0:T(8,128)S(1)}, f32[256,128]{1,0:T(8,128)S(1)}, u32[]{:S(2)}, u32[]{:S(2)}) collective-permute-start(f32[256,128]{1,0:T(8,128)S(1)} %get-tuple-element.19), channel_id=1, source_target_pairs={{0,1},{1,2},{2,3},{3,0},{4,7},{5,4},{6,5},{7,6},{8,9},{9,10},{10,1... | collective-permute-start | bytes 393224 | tf_op jit(solution)/shard_map/ppermute | solution.py:240
  13.3 0.6 %collective-permute-start.3 = (f32[256,128]{1,0:T(8,128)S(1)}, f32[256,128]{1,0:T(8,128)S(1)}, u32[]{:S(2)}, u32[]{:S(2)}) collective-permute-start(f32[256,128]{1,0:T(8,128)S(1)} %get-tuple-element.20), channel_id=1, source_target_pairs={{0,3},{1,0},{2,1},{3,2},{4,5},{5,6},{6,7},{7,4},{8,11},{9,8},{10,9... | collective-permute-start | bytes 393224 | tf_op jit(solution)/shard_map/ppermute | solution.py:240
  13.9 0.4 direct.1.direct_ref
  14.3 3.3 %collective-permute-done.1.q1_ref = f32[256,128]{1,0:T(8,128)S(1)} collective-permute-done((f32[256,128]{1,0:T(8,128)S(1)}, f32[256,128]{1,0:T(8,128)S(1)}, u32[]{:S(2)}, u32[]{:S(2)}) %collective-permute-start.1) | collective-permute-done | bytes 131104 | tf_op jit(solution)/shard_map/ppermute | solution.py:240
  17.6 1.2 %collective-permute-done.2.q2_ref = f32[256,128]{1,0:T(8,128)S(1)} collective-permute-done((f32[256,128]{1,0:T(8,128)S(1)}, f32[256,128]{1,0:T(8,128)S(1)}, u32[]{:S(2)}, u32[]{:S(2)}) %collective-permute-start.2) | collective-permute-done | bytes 131104 | tf_op jit(solution)/shard_map/ppermute | solution.py:240
  18.8 2.4 %collective-permute-done.3.q3_ref = f32[256,128]{1,0:T(8,128)S(1)} collective-permute-done((f32[256,128]{1,0:T(8,128)S(1)}, f32[256,128]{1,0:T(8,128)S(1)}, u32[]{:S(2)}, u32[]{:S(2)}) %collective-permute-start.3) | collective-permute-done | bytes 131104 | tf_op jit(solution)/shard_map/ppermute | solution.py:240
  21.2 0.3 mirror.1
  21.5 2.3 %collective-permute-start.4 = (f32[128,256]{1,0:T(8,128)S(1)}, f32[128,256]{1,0:T(8,128)S(1)}, u32[]{:S(2)}, u32[]{:S(2)}) collective-permute-start(f32[128,256]{1,0:T(8,128)S(1)} %get-tuple-element.22), channel_id=1, source_target_pairs={{0,132},{4,128},{8,140},{12,136},{16,148},{20,144},{24,156},{28,15... | collective-permute-start | bytes 393224 | tf_op jit(solution)/shard_map/ppermute | solution.py:245
  23.8 0.6 %collective-permute-start.5 = (f32[128,256]{1,0:T(8,128)S(1)}, f32[128,256]{1,0:T(8,128)S(1)}, u32[]{:S(2)}, u32[]{:S(2)}) collective-permute-start(f32[128,256]{1,0:T(8,128)S(1)} %get-tuple-element.23), channel_id=1, source_target_pairs={{0,64},{4,192},{8,72},{12,200},{16,80},{20,208},{24,88},{28,216},{... | collective-permute-start | bytes 393224 | tf_op jit(solution)/shard_map/ppermute | solution.py:245
  24.4 0.8 %collective-permute-start.6 = (f32[128,256]{1,0:T(8,128)S(1)}, f32[128,256]{1,0:T(8,128)S(1)}, u32[]{:S(2)}, u32[]{:S(2)}) collective-permute-start(f32[128,256]{1,0:T(8,128)S(1)} %get-tuple-element.24), channel_id=1, source_target_pairs={{0,196},{4,68},{8,204},{12,76},{16,212},{20,84},{24,220},{28,92},{... | collective-permute-start | bytes 393224 | tf_op jit(solution)/shard_map/ppermute | solution.py:245
  25.2 0.0 copy-done
  25.2 0.1 select_reduce_fusion
  25.3 3.5 %collective-permute-done.4.r1_ref = f32[128,256]{1,0:T(8,128)S(1)} collective-permute-done((f32[128,256]{1,0:T(8,128)S(1)}, f32[128,256]{1,0:T(8,128)S(1)}, u32[]{:S(2)}, u32[]{:S(2)}) %collective-permute-start.4) | collective-permute-done | bytes 131104 | tf_op jit(solution)/shard_map/ppermute | solution.py:245
  28.9 2.0 %collective-permute-done.5.r2_ref = f32[128,256]{1,0:T(8,128)S(1)} collective-permute-done((f32[128,256]{1,0:T(8,128)S(1)}, f32[128,256]{1,0:T(8,128)S(1)}, u32[]{:S(2)}, u32[]{:S(2)}) %collective-permute-start.5) | collective-permute-done | bytes 131104 | tf_op jit(solution)/shard_map/ppermute | solution.py:245
  30.9 0.7 %collective-permute-done.6.r3_ref = f32[128,256]{1,0:T(8,128)S(1)} collective-permute-done((f32[128,256]{1,0:T(8,128)S(1)}, f32[128,256]{1,0:T(8,128)S(1)}, u32[]{:S(2)}, u32[]{:S(2)}) %collective-permute-start.6) | collective-permute-done | bytes 131104 | tf_op jit(solution)/shard_map/ppermute | solution.py:245
  31.6 0.7 %gather.1 = f32[8,16,256]{2,1,0:T(8,128)} custom-call(f32[128,256]{1,0:T(8,128)S(1)} %get-tuple-element.21.r0_ref, f32[128,256]{1,0:T(8,128)S(1)} %collective-permute-done.4.r1_ref, f32[128,256]{1,0:T(8,128)S(1)} %collective-permute-done.5.r2_ref, f32[128,256]{1,0:T(8,128)S(1)} %collective-permute-done.6.r3_ref), custom_call_target="tpu_custom_call" | custom-call | tf_op jit(solution)/shard_map/gather/pallas_call | solution.py:179
  32.3 9.5 %all-to-all-start = ((f32[8,16,256]{2,1,0:T(8,128)}), f32[8,16,256]{2,1,0:T(8,128)S(1)}, u32[]{:S(2)}, u32[]{:S(2)}) async-start(f32[8,16,256]{2,1,0:T(8,128)} %gather.1), calls=%async_computation | async-start | bytes 262144 | tf_op jit(solution)/shard_map/all_to_all | solution.py:247
  41.8 0.0 copy-done.1
  41.8 0.2 select_reduce_fusion.3
  42.0 0.1 subtract_subtract_fusion.denom_ref
  42.1 3.4 %all-to-all-done.parts_ref = f32[8,16,256]{2,1,0:T(8,128)S(1)} async-done(((f32[8,16,256]{2,1,0:T(8,128)}), f32[8,16,256]{2,1,0:T(8,128)S(1)}, u32[]{:S(2)}, u32[]{:S(2)}) %all-to-all-start) | async-done | bytes 131104 | tf_op jit(solution)/shard_map/all_to_all | solution.py:247
  45.5 0.8 %finish.1 = f32[16,256]{1,0:T(8,128)} custom-call(f32[8,16,256]{2,1,0:T(8,128)S(1)} %all-to-all-done.parts_ref, f32[16,256]{1,0:T(8,128)S(1)} %subtract_subtract_fusion.denom_ref), custom_call_target="tpu_custom_call" | custom-call | tf_op jit(solution)/shard_map/finish/pallas_call | solution.py:179
  (4 shorter events, 0.0 us)
Async XLA Ops:
  0.0 25.2 %copy-start = (f32[32]{0:T(128)S(1)}, f32[32]{0:T(128)}, u32[]{:S(2)}) copy-start(f32[32]{0:T(128)} %param.8) | copy-start | bytes 388
  5.8 36.0 %copy-start.1 = (f32[32]{0:T(128)S(1)}, f32[32]{0:T(128)}, u32[]{:S(2)}) copy-start(f32[32]{0:T(128)} %param.9) | copy-start | bytes 388
  5.8 4.8 %collective-permute-start = (f32[512,256]{1,0:T(8,128)S(1)}, f32[512,256]{1,0:T(8,128)S(1)}, u32[]{:S(2)}, u32[]{:S(2)}) collective-permute-start(f32[512,256]{1,0:T(8,128)S(1)} %get-tuple-element.16), channel_id=1, source_target_pairs={{0,4},{4,0},{1,5},{5,1},{2,6},{6,2},{3,7},{7,3},{8,12},{12,8},{9,1... | collective-permute-start | bytes 1572872 | tf_op jit(solution)/shard_map/ppermute | solution.py:236
  11.3 6.3 %collective-permute-start.1 = (f32[256,128]{1,0:T(8,128)S(1)}, f32[256,128]{1,0:T(8,128)S(1)}, u32[]{:S(2)}, u32[]{:S(2)}) collective-permute-start(f32[256,128]{1,0:T(8,128)S(1)} %get-tuple-element.18), channel_id=1, source_target_pairs={{0,2},{1,3},{2,0},{3,1},{4,6},{5,7},{6,4},{7,5},{8,10},{9,11},{10,... | collective-permute-start | bytes 393224 | tf_op jit(solution)/shard_map/ppermute | solution.py:240
  12.4 6.3 %collective-permute-start.2 = (f32[256,128]{1,0:T(8,128)S(1)}, f32[256,128]{1,0:T(8,128)S(1)}, u32[]{:S(2)}, u32[]{:S(2)}) collective-permute-start(f32[256,128]{1,0:T(8,128)S(1)} %get-tuple-element.19), channel_id=1, source_target_pairs={{0,1},{1,2},{2,3},{3,0},{4,7},{5,4},{6,5},{7,6},{8,9},{9,10},{10,1... | collective-permute-start | bytes 393224 | tf_op jit(solution)/shard_map/ppermute | solution.py:240
  13.3 7.9 %collective-permute-start.3 = (f32[256,128]{1,0:T(8,128)S(1)}, f32[256,128]{1,0:T(8,128)S(1)}, u32[]{:S(2)}, u32[]{:S(2)}) collective-permute-start(f32[256,128]{1,0:T(8,128)S(1)} %get-tuple-element.20), channel_id=1, source_target_pairs={{0,3},{1,0},{2,1},{3,2},{4,5},{5,6},{6,7},{7,4},{8,11},{9,8},{10,9... | collective-permute-start | bytes 393224 | tf_op jit(solution)/shard_map/ppermute | solution.py:240
  21.5 7.4 %collective-permute-start.4 = (f32[128,256]{1,0:T(8,128)S(1)}, f32[128,256]{1,0:T(8,128)S(1)}, u32[]{:S(2)}, u32[]{:S(2)}) collective-permute-start(f32[128,256]{1,0:T(8,128)S(1)} %get-tuple-element.22), channel_id=1, source_target_pairs={{0,132},{4,128},{8,140},{12,136},{16,148},{20,144},{24,156},{28,15... | collective-permute-start | bytes 393224 | tf_op jit(solution)/shard_map/ppermute | solution.py:245
  23.8 7.1 %collective-permute-start.5 = (f32[128,256]{1,0:T(8,128)S(1)}, f32[128,256]{1,0:T(8,128)S(1)}, u32[]{:S(2)}, u32[]{:S(2)}) collective-permute-start(f32[128,256]{1,0:T(8,128)S(1)} %get-tuple-element.23), channel_id=1, source_target_pairs={{0,64},{4,192},{8,72},{12,200},{16,80},{20,208},{24,88},{28,216},{... | collective-permute-start | bytes 393224 | tf_op jit(solution)/shard_map/ppermute | solution.py:245
  24.4 7.2 %collective-permute-start.6 = (f32[128,256]{1,0:T(8,128)S(1)}, f32[128,256]{1,0:T(8,128)S(1)}, u32[]{:S(2)}, u32[]{:S(2)}) collective-permute-start(f32[128,256]{1,0:T(8,128)S(1)} %get-tuple-element.24), channel_id=1, source_target_pairs={{0,196},{4,68},{8,204},{12,76},{16,212},{20,84},{24,220},{28,92},{... | collective-permute-start | bytes 393224 | tf_op jit(solution)/shard_map/ppermute | solution.py:245
  32.3 13.2 %all-to-all-start = ((f32[8,16,256]{2,1,0:T(8,128)}), f32[8,16,256]{2,1,0:T(8,128)S(1)}, u32[]{:S(2)}, u32[]{:S(2)}) async-start(f32[8,16,256]{2,1,0:T(8,128)} %gather.1), calls=%async_computation | async-start | bytes 262144 | tf_op jit(solution)/shard_map/all_to_all | solution.py:247

commit v5 on v4

--- a/solution.py
+++ b/solution.py
@@ -16,6 +16,7 @@
 CHUNKS = 4
 NY, NZ, NX = 4, 8, 4
 STEPS = (0, 2, 1, 3)
+YSTEPS = (0, 2, 3, 1)
 HALF = 16
 EIGHT = 8
 VIR = ("y", "z", "core")
@@ -106,47 +107,56 @@
             outs[own][pl.ds(a * HALF, HALF), :] = acc[pl.ds(row, HALF), :]
 
 
-def column_order(turned):
-    n = lax.broadcasted_iota(jnp.int32, (256, 256), 0)
-    g = lax.broadcasted_iota(jnp.int32, (256, 256), 1)
-    outer, inner = (g // EIGHT) % EIGHT, g % EIGHT
-    if turned:
-        outer, inner = inner, outer
-    return (n == outer * 32 + EIGHT * (g // 64) + inner).astype(F32).astype(BF16)
-
-
-def split_kernel(keep_ref, recv_ref, own_ref, p1_ref, p2_ref, p3_ref, xbuf, pieces):
-    mirrored = permute_lanes(keep_ref[...] + recv_ref[...], column_order(True))
+def orders_kernel(unused_ref, turned_ref, place_ref, back_ref):
+    s, x = row_set(place("y"), place("core")), place("occ")
+
+    def column(g, transposed):
+        occ = x
+        for n in range(1, NX):
+            occ = jnp.where(g // 64 == n, turn(x, STEPS[n], NX, s), occ)
+        outer, inner = (g // EIGHT) % EIGHT, g % EIGHT
+        if transposed:
+            outer, inner = inner, outer
+        return outer * 32 + EIGHT * occ + inner
+
+    down = lax.broadcasted_iota(jnp.int32, (256, 256), 0)
+    along = lax.broadcasted_iota(jnp.int32, (256, 256), 1)
+    turned_ref[...] = (down == column(along, True)).astype(F32).astype(BF16)
+    place_ref[...] = (down == column(along, False)).astype(F32).astype(BF16)
+    back_ref[...] = (along == column(down, False)).astype(F32).astype(BF16)
+
+
+def split_kernel(keep_ref, recv_ref, turned_ref, own_ref, p1_ref, p2_ref, p3_ref, xbuf):
+    mirrored = permute_lanes(keep_ref[...] + recv_ref[...], turned_ref[...])
     for t in range(2):
         xbuf[t] = mirrored[:, t * 128 : t * 128 + 128]
-    s, x = row_set(place("y"), place("core")), place("occ")
+    s = row_set(place("y"), place("core"))
+    pieces = (own_ref, p1_ref, p2_ref, p3_ref)
     left = lax.broadcasted_iota(jnp.int32, (HALF, 128), 1) < 64
     for a in range(HALF):
         rows = pl.ds(a * HALF, HALF)
         for t in range(2):
             one = xbuf[t, pl.ds(s * 256 + a, HALF, stride=HALF), :]
             two = xbuf[t, pl.ds((1 - s) * 256 + a, HALF, stride=HALF), :]
-            pieces[2 * t, rows, :] = jnp.where(left, one, pltpu.roll(two, 64, 1))
-            pieces[2 * t + 1, rows, :] = jnp.where(left, pltpu.roll(one, 64, 1), two)
-    for k, ref in zip(STEPS, (own_ref, p1_ref, p2_ref, p3_ref)):
-        ref[...] = pieces[turn(x, k, NX, place("core"))]
-
-
-def direct_kernel(keep_ref, recv_ref, out_ref):
-    out_ref[...] = permute_lanes(keep_ref[...] + recv_ref[...], column_order(False))
-
-
-def mirror_kernel(direct_ref, own_ref, q1_ref, q2_ref, q3_ref, o0_ref, o1_ref, o2_ref, o3_ref, pieces, total):
-    x, y, core = place("occ"), place("y"), place("core")
-    for k, ref in zip(STEPS, (own_ref, q1_ref, q2_ref, q3_ref)):
-        pieces[turn(x, -k, NX, core)] = ref[...]
+            pieces[2 * t][rows, :] = jnp.where(left, one, pltpu.roll(two, 64, 1))
+            pieces[2 * t + 1][rows, :] = jnp.where(left, pltpu.roll(one, 64, 1), two)
+
+
+def direct_kernel(keep_ref, recv_ref, place_ref, out_ref):
+    out_ref[...] = permute_lanes(keep_ref[...] + recv_ref[...], place_ref[...])
+
+
+def mirror_kernel(direct_ref, own_ref, q1_ref, q2_ref, q3_ref, o0_ref, o1_ref, o2_ref, o3_ref, total):
+    y, core = place("y"), place("core")
+    arrived = (own_ref, q1_ref, q2_ref, q3_ref)
+    groups = [arrived[STEPS.index((NX - k) % NX)] for k in STEPS]
     left = lax.broadcasted_iota(jnp.int32, (256, 128), 1) < 64
     for t in range(2):
-        even, odd = pieces[2 * t], pieces[2 * t + 1]
+        even, odd = groups[2 * t][...], groups[2 * t + 1][...]
         lanes = pl.ds(t * 128, 128)
         total[0:256, lanes] = direct_ref[0:256, lanes] + jnp.where(left, even, pltpu.roll(odd, 64, 1))
         total[256:512, lanes] = direct_ref[256:512, lanes] + jnp.where(left, pltpu.roll(even, 64, 1), odd)
-    for k, ref in zip(STEPS, (o0_ref, o1_ref, o2_ref, o3_ref)):
+    for k, ref in zip(YSTEPS, (o0_ref, o1_ref, o2_ref, o3_ref)):
         ref[...] = total[pl.ds(pl.multiple_of(turn(y, k, NY, row_set(y, core)) * 128, 128), 128), :]
 
 
@@ -156,14 +166,11 @@
         out_ref[p] = (r0_ref[rows, :] + r1_ref[rows, :]) + (r2_ref[rows, :] + r3_ref[rows, :])
 
 
-def finish_kernel(parts_ref, denom_ref, out_ref):
-    n = lax.broadcasted_iota(jnp.int32, (256, 256), 1)
-    g = lax.broadcasted_iota(jnp.int32, (256, 256), 0)
-    back = (n == ((g // 8) % 8) * 32 + 8 * (g // 64) + g % 8).astype(F32).astype(BF16)
+def finish_kernel(parts_ref, denom_ref, back_ref, out_ref):
     acc = parts_ref[0]
     for z in range(1, NZ):
         acc = acc + parts_ref[z]
-    out_ref[...] = permute_lanes(acc, back) / denom_ref[...]
+    out_ref[...] = permute_lanes(acc, back_ref[...]) / denom_ref[...]
 
 
 def params(mib):
@@ -200,9 +207,14 @@
 
 
 def shift_x(k):
-    return [
-        (core * NX + x, core * NX + (x + (k if core == 0 else -k)) % NX) for core in range(2) for x in range(NX)
-    ]
+    pairs = []
+    for y in range(NY):
+        for core in range(2):
+            s = core ^ (y >= NY // 2)
+            for x in range(NX):
+                to = (x + (k if s == 0 else -k)) % NX
+                pairs.append(((y * 2 + core) * NX + x, (y * 2 + core) * NX + to))
+    return pairs
 
 
 def z_groups():
@@ -234,15 +246,21 @@
         name="ladder",
     )(in_hbm(tile_slot), in_hbm(tiles), in_hbm(amplitudes))
     recv = lax.ppermute(send, "core", [(0, 1), (1, 0)])
-    pieces = kernel_call(
-        split_kernel, "split", [keep, recv], [f32(256, 128)] * 4, [(2, 512, 128), (4, 256, 128)]
+    turned, grouped, back = pl.pallas_call(
+        orders_kernel,
+        in_specs=[pl.BlockSpec(memory_space=pl.ANY)],
+        out_specs=[vmem_spec()] * 3,
+        out_shape=[jax.ShapeDtypeStruct((256, 256), BF16)] * 3,
+        compiler_params=params(8),
+        name="orders",
+    )(keep)
+    pieces = kernel_call(split_kernel, "split", [keep, recv, turned], [f32(256, 128)] * 4, [(2, 512, 128)])
+    moved = [lax.ppermute(pieces[n], ("y", "core", "occ"), shift_x(STEPS[n])) for n in range(1, NX)]
+    direct = kernel_call(direct_kernel, "direct", [keep, recv, grouped], f32(512, 256))
+    own, *others = kernel_call(
+        mirror_kernel, "mirror", [direct, pieces[0], *moved], [f32(128, 256)] * 4, [(512, 256)]
     )
-    moved = [lax.ppermute(pieces[n], ("core", "occ"), shift_x(STEPS[n])) for n in range(1, NX)]
-    direct = kernel_call(direct_kernel, "direct", [keep, recv], f32(512, 256))
-    own, *others = kernel_call(
-        mirror_kernel, "mirror", [direct, pieces[0], *moved], [f32(128, 256)] * 4, [(4, 256, 128), (512, 256)]
-    )
-    moved = [lax.ppermute(others[n - 1], VIR, shift_y(STEPS[n])) for n in range(1, NY)]
+    moved = [lax.ppermute(others[n - 1], VIR, shift_y(YSTEPS[n])) for n in range(1, NY)]
     summed = kernel_call(gather_kernel, "gather", [own, *moved], f32(NZ, HALF, 256))
     parts = lax.all_to_all(summed, VIR, 0, 0, axis_index_groups=z_groups())
 
@@ -256,7 +274,7 @@
     first = pick(vir_energy, jnp.full((HALF,), y * NZ + z, jnp.int32))
     second = pick(vir_energy, core * HALF + row)
     denominator = pair[None, :] - first[:, None] - second[:, None]
-    return kernel_call(finish_kernel, "finish", [parts, denominator], f32(HALF, 256))
+    return kernel_call(finish_kernel, "finish", [parts, denominator, back], f32(HALF, 256))
 
 
 def solution(mesh):

time: 46.5 us -> 45.5 us (0.978)
  the two profiles are of different devices: /device:TPU:1 before, /device:TPU:2 now
where the time goes in v5:
time: 45.5 us; the launch traced here: 45.3 us
  starting transfers between devices  19.7 us (43%)
  waiting for transfers between devices  16.5 us (36%)
  Pallas kernels  8.59 us (19%)
    all_to_all x1, starting transfers between devices, per_device(): parts = lax.all_to_all(summed, VIR, 0, 0, axis_index_groups=z_groups())  10.5 us
    pallas_call x1, Pallas kernels, per_device(): pl.pallas_call(ladder_kernel, in_specs=[pl.BlockSpec(memory_space=pltpu.H...  5.74 us
    ppermute x3, waiting for transfers between devices, per_device(): lax.ppermute(others[n - 1], VIR, shift_y(YSTEPS[n]))  5.65 us
    ppermute x3, waiting for transfers between devices, per_device(): lax.ppermute(pieces[n], ('y', 'core', 'occ'), shift_x(STEPS[n]))  5.33 us
    ppermute x3, starting transfers between devices, per_device(): lax.ppermute(others[n - 1], VIR, shift_y(YSTEPS[n]))  4.88 us
    ppermute x3, starting transfers between devices, per_device(): lax.ppermute(pieces[n], ('y', 'core', 'occ'), shift_x(STEPS[n]))  4.24 us
    all_to_all x1, waiting for transfers between devices, per_device(): parts = lax.all_to_all(summed, VIR, 0, 0, axis_index_groups=z_groups())  3.81 us
    pallas_call x5, Pallas kernels, kernel_call(): pl.pallas_call(body, in_specs=[vmem_spec()] * len(args), out_specs=vmem_s...  2.74 us
  transfers between devices with their start and end apart: 8, of which 6 were waited for; matrix products, arithmetic and copies ran while one was open for 1% of the time, Pallas kernels for 1%

profile of v5, /device:TPU:2, one launch (start us, length us, event | category | flops | bytes accessed | tf_op | source)
XLA Modules:
  0.0 45.3 jit_solution(6326666789408825192)
XLA Ops:
  0.0 5.7 %ladder.1 = (f32[512,256]{1,0:T(8,128)S(1)}, f32[512,256]{1,0:T(8,128)S(1)}) custom-call(s32[64]{0:T(128)} %slot_hbm.1, f32[64,128,128]{2,1,0:T(8,128)} %tiles_hbm.1, f32[4096,256]{1,0:T(8,128)} %amps_hbm.1), custom_call_target="tpu_custom_call" | custom-call | tf_op jit(solution)/shard_map/ladder/pallas_call | solution.py:230
  5.7 0.0 copy-start
  5.8 0.0 copy-start.1
  5.8 0.1 collective-permute-start
  5.9 0.1 orders.1
  6.0 1.8 %collective-permute-done.recv_ref = f32[512,256]{1,0:T(8,128)S(1)} collective-permute-done((f32[512,256]{1,0:T(8,128)S(1)}, f32[512,256]{1,0:T(8,128)S(1)}, u32[]{:S(2)}, u32[]{:S(2)}) %collective-permute-start) | collective-permute-done | bytes 524320 | tf_op jit(solution)/shard_map/ppermute | solution.py:248
  7.8 0.6 %split.1 = (f32[256,128]{1,0:T(8,128)S(1)}, f32[256,128]{1,0:T(8,128)S(1)}, f32[256,128]{1,0:T(8,128)S(1)}, f32[256,128]{1,0:T(8,128)S(1)}) custom-call(f32[512,256]{1,0:T(8,128)S(1)} %get-tuple-element.18.unused_ref.keep_ref, f32[512,256]{1,0:T(8,128)S(1)} %collective-permute-done.recv_ref, bf16[256,256]{1,0:T(8,128)(2,1)S(1)} %get-tuple-element.21.turned_ref), custom_call_target="tpu_custom_call" | custom-call | tf_op jit(solution)/shard_map/split/pallas_call | solution.py:186
  8.4 2.2 %collective-permute-start.1 = (f32[256,128]{1,0:T(8,128)S(1)}, f32[256,128]{1,0:T(8,128)S(1)}, u32[]{:S(2)}, u32[]{:S(2)}) collective-permute-start(f32[256,128]{1,0:T(8,128)S(1)} %get-tuple-element.23), channel_id=1, source_target_pairs={{0,2},{1,3},{2,0},{3,1},{4,6},{5,7},{6,4},{7,5},{64,66},{65,67},{6... | collective-permute-start | bytes 393224 | tf_op jit(solution)/shard_map/ppermute | solution.py:258
  10.6 1.6 %collective-permute-start.2 = (f32[256,128]{1,0:T(8,128)S(1)}, f32[256,128]{1,0:T(8,128)S(1)}, u32[]{:S(2)}, u32[]{:S(2)}) collective-permute-start(f32[256,128]{1,0:T(8,128)S(1)} %get-tuple-element.24), channel_id=1, source_target_pairs={{0,1},{1,2},{2,3},{3,0},{4,7},{5,4},{6,5},{7,6},{64,65},{65,66},{6... | collective-permute-start | bytes 393224 | tf_op jit(solution)/shard_map/ppermute | solution.py:258
  12.2 0.4 collective-permute-start.3
  12.7 0.4 direct.1.direct_ref
  13.1 3.3 %collective-permute-done.1.q1_ref = f32[256,128]{1,0:T(8,128)S(1)} collective-permute-done((f32[256,128]{1,0:T(8,128)S(1)}, f32[256,128]{1,0:T(8,128)S(1)}, u32[]{:S(2)}, u32[]{:S(2)}) %collective-permute-start.1) | collective-permute-done | bytes 131104 | tf_op jit(solution)/shard_map/ppermute | solution.py:258
  16.4 2.0 %collective-permute-done.2.q2_ref = f32[256,128]{1,0:T(8,128)S(1)} collective-permute-done((f32[256,128]{1,0:T(8,128)S(1)}, f32[256,128]{1,0:T(8,128)S(1)}, u32[]{:S(2)}, u32[]{:S(2)}) %collective-permute-start.2) | collective-permute-done | bytes 131104 | tf_op jit(solution)/shard_map/ppermute | solution.py:258
  18.4 0.0 collective-permute-done.3.q3_ref
  18.4 0.2 mirror.1
  18.7 2.9 %collective-permute-start.4 = (f32[128,256]{1,0:T(8,128)S(1)}, f32[128,256]{1,0:T(8,128)S(1)}, u32[]{:S(2)}, u32[]{:S(2)}) collective-permute-start(f32[128,256]{1,0:T(8,128)S(1)} %get-tuple-element.27), channel_id=1, source_target_pairs={{0,132},{4,128},{8,140},{12,136},{16,148},{20,144},{24,156},{28,15... | collective-permute-start | bytes 393224 | tf_op jit(solution)/shard_map/ppermute | solution.py:263
  21.5 1.2 %collective-permute-start.5 = (f32[128,256]{1,0:T(8,128)S(1)}, f32[128,256]{1,0:T(8,128)S(1)}, u32[]{:S(2)}, u32[]{:S(2)}) collective-permute-start(f32[128,256]{1,0:T(8,128)S(1)} %get-tuple-element.28), channel_id=1, source_target_pairs={{0,196},{4,68},{8,204},{12,76},{16,212},{20,84},{24,220},{28,92},{... | collective-permute-start | bytes 393224 | tf_op jit(solution)/shard_map/ppermute | solution.py:263
  22.7 0.8 %collective-permute-start.6 = (f32[128,256]{1,0:T(8,128)S(1)}, f32[128,256]{1,0:T(8,128)S(1)}, u32[]{:S(2)}, u32[]{:S(2)}) collective-permute-start(f32[128,256]{1,0:T(8,128)S(1)} %get-tuple-element.29), channel_id=1, source_target_pairs={{0,64},{4,192},{8,72},{12,200},{16,80},{20,208},{24,88},{28,216},{... | collective-permute-start | bytes 393224 | tf_op jit(solution)/shard_map/ppermute | solution.py:263
  23.5 0.0 copy-done
  23.5 0.1 select_reduce_fusion
  23.6 2.1 %collective-permute-done.4.r1_ref = f32[128,256]{1,0:T(8,128)S(1)} collective-permute-done((f32[128,256]{1,0:T(8,128)S(1)}, f32[128,256]{1,0:T(8,128)S(1)}, u32[]{:S(2)}, u32[]{:S(2)}) %collective-permute-start.4) | collective-permute-done | bytes 131104 | tf_op jit(solution)/shard_map/ppermute | solution.py:263
  25.8 3.5 %collective-permute-done.5.r2_ref = f32[128,256]{1,0:T(8,128)S(1)} collective-permute-done((f32[128,256]{1,0:T(8,128)S(1)}, f32[128,256]{1,0:T(8,128)S(1)}, u32[]{:S(2)}, u32[]{:S(2)}) %collective-permute-start.5) | collective-permute-done | bytes 131104 | tf_op jit(solution)/shard_map/ppermute | solution.py:263
  29.2 0.0 collective-permute-done.6.r3_ref
  29.3 0.7 %gather.1 = f32[8,16,256]{2,1,0:T(8,128)} custom-call(f32[128,256]{1,0:T(8,128)S(1)} %get-tuple-element.26.r0_ref, f32[128,256]{1,0:T(8,128)S(1)} %collective-permute-done.4.r1_ref, f32[128,256]{1,0:T(8,128)S(1)} %collective-permute-done.5.r2_ref, f32[128,256]{1,0:T(8,128)S(1)} %collective-permute-done.6.r3_ref), custom_call_target="tpu_custom_call" | custom-call | tf_op jit(solution)/shard_map/gather/pallas_call | solution.py:186
  29.9 10.5 %all-to-all-start = ((f32[8,16,256]{2,1,0:T(8,128)}), f32[8,16,256]{2,1,0:T(8,128)S(1)}, u32[]{:S(2)}, u32[]{:S(2)}) async-start(f32[8,16,256]{2,1,0:T(8,128)} %gather.1), calls=%async_computation | async-start | bytes 262144 | tf_op jit(solution)/shard_map/all_to_all | solution.py:265
  40.4 0.0 copy-done.1
  40.4 0.2 select_reduce_fusion.3
  40.6 0.1 subtract_subtract_fusion.denom_ref
  40.7 3.8 %all-to-all-done.parts_ref = f32[8,16,256]{2,1,0:T(8,128)S(1)} async-done(((f32[8,16,256]{2,1,0:T(8,128)}), f32[8,16,256]{2,1,0:T(8,128)S(1)}, u32[]{:S(2)}, u32[]{:S(2)}) %all-to-all-start) | async-done | bytes 131104 | tf_op jit(solution)/shard_map/all_to_all | solution.py:265
  44.5 0.8 %finish.1 = f32[16,256]{1,0:T(8,128)} custom-call(f32[8,16,256]{2,1,0:T(8,128)S(1)} %all-to-all-done.parts_ref, f32[16,256]{1,0:T(8,128)S(1)} %subtract_subtract_fusion.denom_ref, bf16[256,256]{1,0:T(8,128)(2,1)S(1)} %get-tuple-element.30.back_ref), custom_call_target="tpu_custom_call" | custom-call | tf_op jit(solution)/shard_map/finish/pallas_call | solution.py:186
  (4 shorter events, 0.0 us)
Async XLA Ops:
  5.7 17.8 %copy-start = (f32[32]{0:T(128)S(1)}, f32[32]{0:T(128)}, u32[]{:S(2)}) copy-start(f32[32]{0:T(128)} %param.8) | copy-start | bytes 388
  5.8 34.7 %copy-start.1 = (f32[32]{0:T(128)S(1)}, f32[32]{0:T(128)}, u32[]{:S(2)}) copy-start(f32[32]{0:T(128)} %param.9) | copy-start | bytes 388
  5.8 2.0 %collective-permute-start = (f32[512,256]{1,0:T(8,128)S(1)}, f32[512,256]{1,0:T(8,128)S(1)}, u32[]{:S(2)}, u32[]{:S(2)}) collective-permute-start(f32[512,256]{1,0:T(8,128)S(1)} %get-tuple-element.19), channel_id=1, source_target_pairs={{0,4},{4,0},{1,5},{5,1},{2,6},{6,2},{3,7},{7,3},{8,12},{12,8},{9,1... | collective-permute-start | bytes 1572872 | tf_op jit(solution)/shard_map/ppermute | solution.py:248
  8.4 8.0 %collective-permute-start.1 = (f32[256,128]{1,0:T(8,128)S(1)}, f32[256,128]{1,0:T(8,128)S(1)}, u32[]{:S(2)}, u32[]{:S(2)}) collective-permute-start(f32[256,128]{1,0:T(8,128)S(1)} %get-tuple-element.23), channel_id=1, source_target_pairs={{0,2},{1,3},{2,0},{3,1},{4,6},{5,7},{6,4},{7,5},{64,66},{65,67},{6... | collective-permute-start | bytes 393224 | tf_op jit(solution)/shard_map/ppermute | solution.py:258
  10.6 7.8 %collective-permute-start.2 = (f32[256,128]{1,0:T(8,128)S(1)}, f32[256,128]{1,0:T(8,128)S(1)}, u32[]{:S(2)}, u32[]{:S(2)}) collective-permute-start(f32[256,128]{1,0:T(8,128)S(1)} %get-tuple-element.24), channel_id=1, source_target_pairs={{0,1},{1,2},{2,3},{3,0},{4,7},{5,4},{6,5},{7,6},{64,65},{65,66},{6... | collective-permute-start | bytes 393224 | tf_op jit(solution)/shard_map/ppermute | solution.py:258
  12.2 6.2 %collective-permute-start.3 = (f32[256,128]{1,0:T(8,128)S(1)}, f32[256,128]{1,0:T(8,128)S(1)}, u32[]{:S(2)}, u32[]{:S(2)}) collective-permute-start(f32[256,128]{1,0:T(8,128)S(1)} %get-tuple-element.25), channel_id=1, source_target_pairs={{0,3},{1,0},{2,1},{3,2},{4,5},{5,6},{6,7},{7,4},{64,67},{65,64},{6... | collective-permute-start | bytes 393224 | tf_op jit(solution)/shard_map/ppermute | solution.py:258
  18.7 7.1 %collective-permute-start.4 = (f32[128,256]{1,0:T(8,128)S(1)}, f32[128,256]{1,0:T(8,128)S(1)}, u32[]{:S(2)}, u32[]{:S(2)}) collective-permute-start(f32[128,256]{1,0:T(8,128)S(1)} %get-tuple-element.27), channel_id=1, source_target_pairs={{0,132},{4,128},{8,140},{12,136},{16,148},{20,144},{24,156},{28,15... | collective-permute-start | bytes 393224 | tf_op jit(solution)/shard_map/ppermute | solution.py:263
  21.5 7.7 %collective-permute-start.5 = (f32[128,256]{1,0:T(8,128)S(1)}, f32[128,256]{1,0:T(8,128)S(1)}, u32[]{:S(2)}, u32[]{:S(2)}) collective-permute-start(f32[128,256]{1,0:T(8,128)S(1)} %get-tuple-element.28), channel_id=1, source_target_pairs={{0,196},{4,68},{8,204},{12,76},{16,212},{20,84},{24,220},{28,92},{... | collective-permute-start | bytes 393224 | tf_op jit(solution)/shard_map/ppermute | solution.py:263
  22.7 6.5 %collective-permute-start.6 = (f32[128,256]{1,0:T(8,128)S(1)}, f32[128,256]{1,0:T(8,128)S(1)}, u32[]{:S(2)}, u32[]{:S(2)}) collective-permute-start(f32[128,256]{1,0:T(8,128)S(1)} %get-tuple-element.29), channel_id=1, source_target_pairs={{0,64},{4,192},{8,72},{12,200},{16,80},{20,208},{24,88},{28,216},{... | collective-permute-start | bytes 393224 | tf_op jit(solution)/shard_map/ppermute | solution.py:263
  29.9 14.5 %all-to-all-start = ((f32[8,16,256]{2,1,0:T(8,128)}), f32[8,16,256]{2,1,0:T(8,128)S(1)}, u32[]{:S(2)}, u32[]{:S(2)}) async-start(f32[8,16,256]{2,1,0:T(8,128)} %gather.1), calls=%async_computation | async-start | bytes 262144 | tf_op jit(solution)/shard_map/all_to_all | solution.py:265

commit v6 on v5

--- a/solution.py
+++ b/solution.py
@@ -20,7 +20,7 @@
 HALF = 16
 EIGHT = 8
 VIR = ("y", "z", "core")
-Z_ORDER = (4, 5, 6, 7, 0, 1, 2, 3)
+Z_ORDER = (4, 3, 5, 2, 6, 1, 7, 0)
 
 
 def vmem_spec():

time: 45.5 us -> 45.4 us (level)
  no operation moved by 1% of the time
where the time goes in v6:
time: 45.4 us; the launch traced here: 45.2 us
  starting transfers between devices  19.7 us (43%)
  waiting for transfers between devices  16.5 us (36%)
  Pallas kernels  8.59 us (19%)
    all_to_all x1, starting transfers between devices, per_device(): parts = lax.all_to_all(summed, VIR, 0, 0, axis_index_groups=z_groups())  10.5 us
    pallas_call x1, Pallas kernels, per_device(): pl.pallas_call(ladder_kernel, in_specs=[pl.BlockSpec(memory_space=pltpu.H...  5.74 us
    ppermute x3, waiting for transfers between devices, per_device(): lax.ppermute(others[n - 1], VIR, shift_y(YSTEPS[n]))  5.65 us
    ppermute x3, waiting for transfers between devices, per_device(): lax.ppermute(pieces[n], ('y', 'core', 'occ'), shift_x(STEPS[n]))  5.33 us
    ppermute x3, starting transfers between devices, per_device(): lax.ppermute(others[n - 1], VIR, shift_y(YSTEPS[n]))  4.88 us
    ppermute x3, starting transfers between devices, per_device(): lax.ppermute(pieces[n], ('y', 'core', 'occ'), shift_x(STEPS[n]))  4.24 us
    all_to_all x1, waiting for transfers between devices, per_device(): parts = lax.all_to_all(summed, VIR, 0, 0, axis_index_groups=z_groups())  3.74 us
    pallas_call x5, Pallas kernels, kernel_call(): pl.pallas_call(body, in_specs=[vmem_spec()] * len(args), out_specs=vmem_s...  2.74 us
  transfers between devices with their start and end apart: 8, of which 6 were waited for; matrix products, arithmetic and copies ran while one was open for 1% of the time, Pallas kernels for 1%

profile of v6, /device:TPU:2, one launch (start us, length us, event | category | flops | bytes accessed | tf_op | source)
XLA Modules:
  0.0 45.2 jit_solution(9836978116543740384)
XLA Ops:
  0.0 5.7 %ladder.1 = (f32[512,256]{1,0:T(8,128)S(1)}, f32[512,256]{1,0:T(8,128)S(1)}) custom-call(s32[64]{0:T(128)} %slot_hbm.1, f32[64,128,128]{2,1,0:T(8,128)} %tiles_hbm.1, f32[4096,256]{1,0:T(8,128)} %amps_hbm.1), custom_call_target="tpu_custom_call" | custom-call | tf_op jit(solution)/shard_map/ladder/pallas_call | solution.py:230
  5.7 0.0 copy-start
  5.8 0.0 copy-start.1
  5.8 0.1 collective-permute-start
  5.9 0.1 orders.1
  6.0 1.8 %collective-permute-done.recv_ref = f32[512,256]{1,0:T(8,128)S(1)} collective-permute-done((f32[512,256]{1,0:T(8,128)S(1)}, f32[512,256]{1,0:T(8,128)S(1)}, u32[]{:S(2)}, u32[]{:S(2)}) %collective-permute-start) | collective-permute-done | bytes 524320 | tf_op jit(solution)/shard_map/ppermute | solution.py:248
  7.8 0.6 %split.1 = (f32[256,128]{1,0:T(8,128)S(1)}, f32[256,128]{1,0:T(8,128)S(1)}, f32[256,128]{1,0:T(8,128)S(1)}, f32[256,128]{1,0:T(8,128)S(1)}) custom-call(f32[512,256]{1,0:T(8,128)S(1)} %get-tuple-element.18.unused_ref.keep_ref, f32[512,256]{1,0:T(8,128)S(1)} %collective-permute-done.recv_ref, bf16[256,256]{1,0:T(8,128)(2,1)S(1)} %get-tuple-element.21.turned_ref), custom_call_target="tpu_custom_call" | custom-call | tf_op jit(solution)/shard_map/split/pallas_call | solution.py:186
  8.4 2.2 %collective-permute-start.1 = (f32[256,128]{1,0:T(8,128)S(1)}, f32[256,128]{1,0:T(8,128)S(1)}, u32[]{:S(2)}, u32[]{:S(2)}) collective-permute-start(f32[256,128]{1,0:T(8,128)S(1)} %get-tuple-element.23), channel_id=1, source_target_pairs={{0,2},{1,3},{2,0},{3,1},{4,6},{5,7},{6,4},{7,5},{64,66},{65,67},{6... | collective-permute-start | bytes 393224 | tf_op jit(solution)/shard_map/ppermute | solution.py:258
  10.6 1.6 %collective-permute-start.2 = (f32[256,128]{1,0:T(8,128)S(1)}, f32[256,128]{1,0:T(8,128)S(1)}, u32[]{:S(2)}, u32[]{:S(2)}) collective-permute-start(f32[256,128]{1,0:T(8,128)S(1)} %get-tuple-element.24), channel_id=1, source_target_pairs={{0,1},{1,2},{2,3},{3,0},{4,7},{5,4},{6,5},{7,6},{64,65},{65,66},{6... | collective-permute-start | bytes 393224 | tf_op jit(solution)/shard_map/ppermute | solution.py:258
  12.2 0.4 collective-permute-start.3
  12.7 0.4 direct.1.direct_ref
  13.1 3.3 %collective-permute-done.1.q1_ref = f32[256,128]{1,0:T(8,128)S(1)} collective-permute-done((f32[256,128]{1,0:T(8,128)S(1)}, f32[256,128]{1,0:T(8,128)S(1)}, u32[]{:S(2)}, u32[]{:S(2)}) %collective-permute-start.1) | collective-permute-done | bytes 131104 | tf_op jit(solution)/shard_map/ppermute | solution.py:258
  16.4 2.0 %collective-permute-done.2.q2_ref = f32[256,128]{1,0:T(8,128)S(1)} collective-permute-done((f32[256,128]{1,0:T(8,128)S(1)}, f32[256,128]{1,0:T(8,128)S(1)}, u32[]{:S(2)}, u32[]{:S(2)}) %collective-permute-start.2) | collective-permute-done | bytes 131104 | tf_op jit(solution)/shard_map/ppermute | solution.py:258
  18.4 0.0 collective-permute-done.3.q3_ref
  18.4 0.2 mirror.1
  18.7 2.9 %collective-permute-start.4 = (f32[128,256]{1,0:T(8,128)S(1)}, f32[128,256]{1,0:T(8,128)S(1)}, u32[]{:S(2)}, u32[]{:S(2)}) collective-permute-start(f32[128,256]{1,0:T(8,128)S(1)} %get-tuple-element.27), channel_id=1, source_target_pairs={{0,132},{4,128},{8,140},{12,136},{16,148},{20,144},{24,156},{28,15... | collective-permute-start | bytes 393224 | tf_op jit(solution)/shard_map/ppermute | solution.py:263
  21.5 1.2 %collective-permute-start.5 = (f32[128,256]{1,0:T(8,128)S(1)}, f32[128,256]{1,0:T(8,128)S(1)}, u32[]{:S(2)}, u32[]{:S(2)}) collective-permute-start(f32[128,256]{1,0:T(8,128)S(1)} %get-tuple-element.28), channel_id=1, source_target_pairs={{0,196},{4,68},{8,204},{12,76},{16,212},{20,84},{24,220},{28,92},{... | collective-permute-start | bytes 393224 | tf_op jit(solution)/shard_map/ppermute | solution.py:263
  22.7 0.8 %collective-permute-start.6 = (f32[128,256]{1,0:T(8,128)S(1)}, f32[128,256]{1,0:T(8,128)S(1)}, u32[]{:S(2)}, u32[]{:S(2)}) collective-permute-start(f32[128,256]{1,0:T(8,128)S(1)} %get-tuple-element.29), channel_id=1, source_target_pairs={{0,64},{4,192},{8,72},{12,200},{16,80},{20,208},{24,88},{28,216},{... | collective-permute-start | bytes 393224 | tf_op jit(solution)/shard_map/ppermute | solution.py:263
  23.5 0.0 copy-done
  23.5 0.1 select_reduce_fusion
  23.6 2.1 %collective-permute-done.4.r1_ref = f32[128,256]{1,0:T(8,128)S(1)} collective-permute-done((f32[128,256]{1,0:T(8,128)S(1)}, f32[128,256]{1,0:T(8,128)S(1)}, u32[]{:S(2)}, u32[]{:S(2)}) %collective-permute-start.4) | collective-permute-done | bytes 131104 | tf_op jit(solution)/shard_map/ppermute | solution.py:263
  25.8 3.5 %collective-permute-done.5.r2_ref = f32[128,256]{1,0:T(8,128)S(1)} collective-permute-done((f32[128,256]{1,0:T(8,128)S(1)}, f32[128,256]{1,0:T(8,128)S(1)}, u32[]{:S(2)}, u32[]{:S(2)}) %collective-permute-start.5) | collective-permute-done | bytes 131104 | tf_op jit(solution)/shard_map/ppermute | solution.py:263
  29.2 0.0 collective-permute-done.6.r3_ref
  29.3 0.7 %gather.1 = f32[8,16,256]{2,1,0:T(8,128)} custom-call(f32[128,256]{1,0:T(8,128)S(1)} %get-tuple-element.26.r0_ref, f32[128,256]{1,0:T(8,128)S(1)} %collective-permute-done.4.r1_ref, f32[128,256]{1,0:T(8,128)S(1)} %collective-permute-done.5.r2_ref, f32[128,256]{1,0:T(8,128)S(1)} %collective-permute-done.6.r3_ref), custom_call_target="tpu_custom_call" | custom-call | tf_op jit(solution)/shard_map/gather/pallas_call | solution.py:186
  29.9 10.5 %all-to-all-start = ((f32[8,16,256]{2,1,0:T(8,128)}), f32[8,16,256]{2,1,0:T(8,128)S(1)}, u32[]{:S(2)}, u32[]{:S(2)}) async-start(f32[8,16,256]{2,1,0:T(8,128)} %gather.1), calls=%async_computation | async-start | bytes 262144 | tf_op jit(solution)/shard_map/all_to_all | solution.py:265
  40.4 0.0 copy-done.1
  40.4 0.2 select_reduce_fusion.3
  40.6 0.1 subtract_subtract_fusion.denom_ref
  40.7 3.7 %all-to-all-done.parts_ref = f32[8,16,256]{2,1,0:T(8,128)S(1)} async-done(((f32[8,16,256]{2,1,0:T(8,128)}), f32[8,16,256]{2,1,0:T(8,128)S(1)}, u32[]{:S(2)}, u32[]{:S(2)}) %all-to-all-start) | async-done | bytes 131104 | tf_op jit(solution)/shard_map/all_to_all | solution.py:265
  44.4 0.8 %finish.1 = f32[16,256]{1,0:T(8,128)} custom-call(f32[8,16,256]{2,1,0:T(8,128)S(1)} %all-to-all-done.parts_ref, f32[16,256]{1,0:T(8,128)S(1)} %subtract_subtract_fusion.denom_ref, bf16[256,256]{1,0:T(8,128)(2,1)S(1)} %get-tuple-element.30.back_ref), custom_call_target="tpu_custom_call" | custom-call | tf_op jit(solution)/shard_map/finish/pallas_call | solution.py:186
  (4 shorter events, 0.0 us)
Async XLA Ops:
  5.7 17.8 %copy-start = (f32[32]{0:T(128)S(1)}, f32[32]{0:T(128)}, u32[]{:S(2)}) copy-start(f32[32]{0:T(128)} %param.8) | copy-start | bytes 388
  5.8 34.7 %copy-start.1 = (f32[32]{0:T(128)S(1)}, f32[32]{0:T(128)}, u32[]{:S(2)}) copy-start(f32[32]{0:T(128)} %param.9) | copy-start | bytes 388
  5.8 2.0 %collective-permute-start = (f32[512,256]{1,0:T(8,128)S(1)}, f32[512,256]{1,0:T(8,128)S(1)}, u32[]{:S(2)}, u32[]{:S(2)}) collective-permute-start(f32[512,256]{1,0:T(8,128)S(1)} %get-tuple-element.19), channel_id=1, source_target_pairs={{0,4},{4,0},{1,5},{5,1},{2,6},{6,2},{3,7},{7,3},{8,12},{12,8},{9,1... | collective-permute-start | bytes 1572872 | tf_op jit(solution)/shard_map/ppermute | solution.py:248
  8.4 8.0 %collective-permute-start.1 = (f32[256,128]{1,0:T(8,128)S(1)}, f32[256,128]{1,0:T(8,128)S(1)}, u32[]{:S(2)}, u32[]{:S(2)}) collective-permute-start(f32[256,128]{1,0:T(8,128)S(1)} %get-tuple-element.23), channel_id=1, source_target_pairs={{0,2},{1,3},{2,0},{3,1},{4,6},{5,7},{6,4},{7,5},{64,66},{65,67},{6... | collective-permute-start | bytes 393224 | tf_op jit(solution)/shard_map/ppermute | solution.py:258
  10.6 7.8 %collective-permute-start.2 = (f32[256,128]{1,0:T(8,128)S(1)}, f32[256,128]{1,0:T(8,128)S(1)}, u32[]{:S(2)}, u32[]{:S(2)}) collective-permute-start(f32[256,128]{1,0:T(8,128)S(1)} %get-tuple-element.24), channel_id=1, source_target_pairs={{0,1},{1,2},{2,3},{3,0},{4,7},{5,4},{6,5},{7,6},{64,65},{65,66},{6... | collective-permute-start | bytes 393224 | tf_op jit(solution)/shard_map/ppermute | solution.py:258
  12.2 6.2 %collective-permute-start.3 = (f32[256,128]{1,0:T(8,128)S(1)}, f32[256,128]{1,0:T(8,128)S(1)}, u32[]{:S(2)}, u32[]{:S(2)}) collective-permute-start(f32[256,128]{1,0:T(8,128)S(1)} %get-tuple-element.25), channel_id=1, source_target_pairs={{0,3},{1,0},{2,1},{3,2},{4,5},{5,6},{6,7},{7,4},{64,67},{65,64},{6... | collective-permute-start | bytes 393224 | tf_op jit(solution)/shard_map/ppermute | solution.py:258
  18.7 7.1 %collective-permute-start.4 = (f32[128,256]{1,0:T(8,128)S(1)}, f32[128,256]{1,0:T(8,128)S(1)}, u32[]{:S(2)}, u32[]{:S(2)}) collective-permute-start(f32[128,256]{1,0:T(8,128)S(1)} %get-tuple-element.27), channel_id=1, source_target_pairs={{0,132},{4,128},{8,140},{12,136},{16,148},{20,144},{24,156},{28,15... | collective-permute-start | bytes 393224 | tf_op jit(solution)/shard_map/ppermute | solution.py:263
  21.5 7.7 %collective-permute-start.5 = (f32[128,256]{1,0:T(8,128)S(1)}, f32[128,256]{1,0:T(8,128)S(1)}, u32[]{:S(2)}, u32[]{:S(2)}) collective-permute-start(f32[128,256]{1,0:T(8,128)S(1)} %get-tuple-element.28), channel_id=1, source_target_pairs={{0,196},{4,68},{8,204},{12,76},{16,212},{20,84},{24,220},{28,92},{... | collective-permute-start | bytes 393224 | tf_op jit(solution)/shard_map/ppermute | solution.py:263
  22.7 6.5 %collective-permute-start.6 = (f32[128,256]{1,0:T(8,128)S(1)}, f32[128,256]{1,0:T(8,128)S(1)}, u32[]{:S(2)}, u32[]{:S(2)}) collective-permute-start(f32[128,256]{1,0:T(8,128)S(1)} %get-tuple-element.29), channel_id=1, source_target_pairs={{0,64},{4,192},{8,72},{12,200},{16,80},{20,208},{24,88},{28,216},{... | collective-permute-start | bytes 393224 | tf_op jit(solution)/shard_map/ppermute | solution.py:263
  29.9 14.5 %all-to-all-start = ((f32[8,16,256]{2,1,0:T(8,128)}), f32[8,16,256]{2,1,0:T(8,128)S(1)}, u32[]{:S(2)}, u32[]{:S(2)}) async-start(f32[8,16,256]{2,1,0:T(8,128)} %gather.1), calls=%async_computation | async-start | bytes 262144 | tf_op jit(solution)/shard_map/all_to_all | solution.py:265

commit v7 on v6

--- a/solution.py
+++ b/solution.py
@@ -170,7 +170,10 @@
     acc = parts_ref[0]
     for z in range(1, NZ):
         acc = acc + parts_ref[z]
-    out_ref[...] = permute_lanes(acc, back_ref[...]) / denom_ref[...]
+    top, mid, low = split3(acc)
+    terms = jnp.dot(jnp.concatenate([low, mid, top], axis=0), back_ref[...], preferred_element_type=F32)
+    total = (terms[0:HALF] + terms[HALF : 2 * HALF]) + terms[2 * HALF : 3 * HALF]
+    out_ref[...] = total / denom_ref[...]
 
 
 def params(mib):

time: 45.4 us -> 45.4 us (level)
  no operation moved by 1% of the time
where the time goes in v7:
time: 45.4 us; the launch traced here: 45.2 us
  starting transfers between devices  19.7 us (43%)
  waiting for transfers between devices  16.5 us (36%)
  Pallas kernels  8.57 us (19%)
    all_to_all x1, starting transfers between devices, per_device(): parts = lax.all_to_all(summed, VIR, 0, 0, axis_index_groups=z_groups())  10.5 us
    pallas_call x1, Pallas kernels, per_device(): pl.pallas_call(ladder_kernel, in_specs=[pl.BlockSpec(memory_space=pltpu.H...  5.74 us
    ppermute x3, waiting for transfers between devices, per_device(): lax.ppermute(others[n - 1], VIR, shift_y(YSTEPS[n]))  5.65 us
    ppermute x3, waiting for transfers between devices, per_device(): lax.ppermute(pieces[n], ('y', 'core', 'occ'), shift_x(STEPS[n]))  5.33 us
    ppermute x3, starting transfers between devices, per_device(): lax.ppermute(others[n - 1], VIR, shift_y(YSTEPS[n]))  4.88 us
    ppermute x3, starting transfers between devices, per_device(): lax.ppermute(pieces[n], ('y', 'core', 'occ'), shift_x(STEPS[n]))  4.24 us
    all_to_all x1, waiting for transfers between devices, per_device(): parts = lax.all_to_all(summed, VIR, 0, 0, axis_index_groups=z_groups())  3.74 us
    pallas_call x5, Pallas kernels, kernel_call(): pl.pallas_call(body, in_specs=[vmem_spec()] * len(args), out_specs=vmem_s...  2.71 us
  transfers between devices with their start and end apart: 8, of which 6 were waited for; matrix products, arithmetic and copies ran while one was open for 1% of the time, Pallas kernels for 1%

profile of v7, /device:TPU:2, one launch (start us, length us, event | category | flops | bytes accessed | tf_op | source)
XLA Modules:
  0.0 45.2 jit_solution(8529294222143671429)
XLA Ops:
  0.0 5.7 %ladder.1 = (f32[512,256]{1,0:T(8,128)S(1)}, f32[512,256]{1,0:T(8,128)S(1)}) custom-call(s32[64]{0:T(128)} %slot_hbm.1, f32[64,128,128]{2,1,0:T(8,128)} %tiles_hbm.1, f32[4096,256]{1,0:T(8,128)} %amps_hbm.1), custom_call_target="tpu_custom_call" | custom-call | tf_op jit(solution)/shard_map/ladder/pallas_call | solution.py:233
  5.7 0.0 copy-start
  5.8 0.0 copy-start.1
  5.8 0.1 collective-permute-start
  5.9 0.1 orders.1
  6.0 1.8 %collective-permute-done.recv_ref = f32[512,256]{1,0:T(8,128)S(1)} collective-permute-done((f32[512,256]{1,0:T(8,128)S(1)}, f32[512,256]{1,0:T(8,128)S(1)}, u32[]{:S(2)}, u32[]{:S(2)}) %collective-permute-start) | collective-permute-done | bytes 524320 | tf_op jit(solution)/shard_map/ppermute | solution.py:251
  7.8 0.6 %split.1 = (f32[256,128]{1,0:T(8,128)S(1)}, f32[256,128]{1,0:T(8,128)S(1)}, f32[256,128]{1,0:T(8,128)S(1)}, f32[256,128]{1,0:T(8,128)S(1)}) custom-call(f32[512,256]{1,0:T(8,128)S(1)} %get-tuple-element.18.unused_ref.keep_ref, f32[512,256]{1,0:T(8,128)S(1)} %collective-permute-done.recv_ref, bf16[256,256]{1,0:T(8,128)(2,1)S(1)} %get-tuple-element.21.turned_ref), custom_call_target="tpu_custom_call" | custom-call | tf_op jit(solution)/shard_map/split/pallas_call | solution.py:189
  8.4 2.2 %collective-permute-start.1 = (f32[256,128]{1,0:T(8,128)S(1)}, f32[256,128]{1,0:T(8,128)S(1)}, u32[]{:S(2)}, u32[]{:S(2)}) collective-permute-start(f32[256,128]{1,0:T(8,128)S(1)} %get-tuple-element.23), channel_id=1, source_target_pairs={{0,2},{1,3},{2,0},{3,1},{4,6},{5,7},{6,4},{7,5},{64,66},{65,67},{6... | collective-permute-start | bytes 393224 | tf_op jit(solution)/shard_map/ppermute | solution.py:261
  10.6 1.6 %collective-permute-start.2 = (f32[256,128]{1,0:T(8,128)S(1)}, f32[256,128]{1,0:T(8,128)S(1)}, u32[]{:S(2)}, u32[]{:S(2)}) collective-permute-start(f32[256,128]{1,0:T(8,128)S(1)} %get-tuple-element.24), channel_id=1, source_target_pairs={{0,1},{1,2},{2,3},{3,0},{4,7},{5,4},{6,5},{7,6},{64,65},{65,66},{6... | collective-permute-start | bytes 393224 | tf_op jit(solution)/shard_map/ppermute | solution.py:261
  12.2 0.4 collective-permute-start.3
  12.7 0.4 direct.1.direct_ref
  13.1 3.3 %collective-permute-done.1.q1_ref = f32[256,128]{1,0:T(8,128)S(1)} collective-permute-done((f32[256,128]{1,0:T(8,128)S(1)}, f32[256,128]{1,0:T(8,128)S(1)}, u32[]{:S(2)}, u32[]{:S(2)}) %collective-permute-start.1) | collective-permute-done | bytes 131104 | tf_op jit(solution)/shard_map/ppermute | solution.py:261
  16.4 2.0 %collective-permute-done.2.q2_ref = f32[256,128]{1,0:T(8,128)S(1)} collective-permute-done((f32[256,128]{1,0:T(8,128)S(1)}, f32[256,128]{1,0:T(8,128)S(1)}, u32[]{:S(2)}, u32[]{:S(2)}) %collective-permute-start.2) | collective-permute-done | bytes 131104 | tf_op jit(solution)/shard_map/ppermute | solution.py:261
  18.4 0.0 collective-permute-done.3.q3_ref
  18.4 0.2 mirror.1
  18.7 2.9 %collective-permute-start.4 = (f32[128,256]{1,0:T(8,128)S(1)}, f32[128,256]{1,0:T(8,128)S(1)}, u32[]{:S(2)}, u32[]{:S(2)}) collective-permute-start(f32[128,256]{1,0:T(8,128)S(1)} %get-tuple-element.27), channel_id=1, source_target_pairs={{0,132},{4,128},{8,140},{12,136},{16,148},{20,144},{24,156},{28,15... | collective-permute-start | bytes 393224 | tf_op jit(solution)/shard_map/ppermute | solution.py:266
  21.5 1.2 %collective-permute-start.5 = (f32[128,256]{1,0:T(8,128)S(1)}, f32[128,256]{1,0:T(8,128)S(1)}, u32[]{:S(2)}, u32[]{:S(2)}) collective-permute-start(f32[128,256]{1,0:T(8,128)S(1)} %get-tuple-element.28), channel_id=1, source_target_pairs={{0,196},{4,68},{8,204},{12,76},{16,212},{20,84},{24,220},{28,92},{... | collective-permute-start | bytes 393224 | tf_op jit(solution)/shard_map/ppermute | solution.py:266
  22.7 0.8 %collective-permute-start.6 = (f32[128,256]{1,0:T(8,128)S(1)}, f32[128,256]{1,0:T(8,128)S(1)}, u32[]{:S(2)}, u32[]{:S(2)}) collective-permute-start(f32[128,256]{1,0:T(8,128)S(1)} %get-tuple-element.29), channel_id=1, source_target_pairs={{0,64},{4,192},{8,72},{12,200},{16,80},{20,208},{24,88},{28,216},{... | collective-permute-start | bytes 393224 | tf_op jit(solution)/shard_map/ppermute | solution.py:266
  23.5 0.0 copy-done
  23.5 0.1 select_reduce_fusion
  23.6 2.1 %collective-permute-done.4.r1_ref = f32[128,256]{1,0:T(8,128)S(1)} collective-permute-done((f32[128,256]{1,0:T(8,128)S(1)}, f32[128,256]{1,0:T(8,128)S(1)}, u32[]{:S(2)}, u32[]{:S(2)}) %collective-permute-start.4) | collective-permute-done | bytes 131104 | tf_op jit(solution)/shard_map/ppermute | solution.py:266
  25.8 3.5 %collective-permute-done.5.r2_ref = f32[128,256]{1,0:T(8,128)S(1)} collective-permute-done((f32[128,256]{1,0:T(8,128)S(1)}, f32[128,256]{1,0:T(8,128)S(1)}, u32[]{:S(2)}, u32[]{:S(2)}) %collective-permute-start.5) | collective-permute-done | bytes 131104 | tf_op jit(solution)/shard_map/ppermute | solution.py:266
  29.2 0.0 collective-permute-done.6.r3_ref
  29.3 0.7 %gather.1 = f32[8,16,256]{2,1,0:T(8,128)} custom-call(f32[128,256]{1,0:T(8,128)S(1)} %get-tuple-element.26.r0_ref, f32[128,256]{1,0:T(8,128)S(1)} %collective-permute-done.4.r1_ref, f32[128,256]{1,0:T(8,128)S(1)} %collective-permute-done.5.r2_ref, f32[128,256]{1,0:T(8,128)S(1)} %collective-permute-done.6.r3_ref), custom_call_target="tpu_custom_call" | custom-call | tf_op jit(solution)/shard_map/gather/pallas_call | solution.py:189
  29.9 10.5 %all-to-all-start = ((f32[8,16,256]{2,1,0:T(8,128)}), f32[8,16,256]{2,1,0:T(8,128)S(1)}, u32[]{:S(2)}, u32[]{:S(2)}) async-start(f32[8,16,256]{2,1,0:T(8,128)} %gather.1), calls=%async_computation | async-start | bytes 262144 | tf_op jit(solution)/shard_map/all_to_all | solution.py:268
  40.4 0.0 copy-done.1
  40.4 0.2 select_reduce_fusion.3
  40.6 0.1 subtract_subtract_fusion.denom_ref
  40.7 3.7 %all-to-all-done.parts_ref = f32[8,16,256]{2,1,0:T(8,128)S(1)} async-done(((f32[8,16,256]{2,1,0:T(8,128)}), f32[8,16,256]{2,1,0:T(8,128)S(1)}, u32[]{:S(2)}, u32[]{:S(2)}) %all-to-all-start) | async-done | bytes 131104 | tf_op jit(solution)/shard_map/all_to_all | solution.py:268
  44.4 0.8 %finish.1 = f32[16,256]{1,0:T(8,128)} custom-call(f32[8,16,256]{2,1,0:T(8,128)S(1)} %all-to-all-done.parts_ref, f32[16,256]{1,0:T(8,128)S(1)} %subtract_subtract_fusion.denom_ref, bf16[256,256]{1,0:T(8,128)(2,1)S(1)} %get-tuple-element.30.back_ref), custom_call_target="tpu_custom_call" | custom-call | tf_op jit(solution)/shard_map/finish/pallas_call | solution.py:189
  (4 shorter events, 0.0 us)
Async XLA Ops:
  5.7 17.8 %copy-start = (f32[32]{0:T(128)S(1)}, f32[32]{0:T(128)}, u32[]{:S(2)}) copy-start(f32[32]{0:T(128)} %param.8) | copy-start | bytes 388
  5.8 34.7 %copy-start.1 = (f32[32]{0:T(128)S(1)}, f32[32]{0:T(128)}, u32[]{:S(2)}) copy-start(f32[32]{0:T(128)} %param.9) | copy-start | bytes 388
  5.8 2.0 %collective-permute-start = (f32[512,256]{1,0:T(8,128)S(1)}, f32[512,256]{1,0:T(8,128)S(1)}, u32[]{:S(2)}, u32[]{:S(2)}) collective-permute-start(f32[512,256]{1,0:T(8,128)S(1)} %get-tuple-element.19), channel_id=1, source_target_pairs={{0,4},{4,0},{1,5},{5,1},{2,6},{6,2},{3,7},{7,3},{8,12},{12,8},{9,1... | collective-permute-start | bytes 1572872 | tf_op jit(solution)/shard_map/ppermute | solution.py:251
  8.4 8.0 %collective-permute-start.1 = (f32[256,128]{1,0:T(8,128)S(1)}, f32[256,128]{1,0:T(8,128)S(1)}, u32[]{:S(2)}, u32[]{:S(2)}) collective-permute-start(f32[256,128]{1,0:T(8,128)S(1)} %get-tuple-element.23), channel_id=1, source_target_pairs={{0,2},{1,3},{2,0},{3,1},{4,6},{5,7},{6,4},{7,5},{64,66},{65,67},{6... | collective-permute-start | bytes 393224 | tf_op jit(solution)/shard_map/ppermute | solution.py:261
  10.6 7.8 %collective-permute-start.2 = (f32[256,128]{1,0:T(8,128)S(1)}, f32[256,128]{1,0:T(8,128)S(1)}, u32[]{:S(2)}, u32[]{:S(2)}) collective-permute-start(f32[256,128]{1,0:T(8,128)S(1)} %get-tuple-element.24), channel_id=1, source_target_pairs={{0,1},{1,2},{2,3},{3,0},{4,7},{5,4},{6,5},{7,6},{64,65},{65,66},{6... | collective-permute-start | bytes 393224 | tf_op jit(solution)/shard_map/ppermute | solution.py:261
  12.2 6.2 %collective-permute-start.3 = (f32[256,128]{1,0:T(8,128)S(1)}, f32[256,128]{1,0:T(8,128)S(1)}, u32[]{:S(2)}, u32[]{:S(2)}) collective-permute-start(f32[256,128]{1,0:T(8,128)S(1)} %get-tuple-element.25), channel_id=1, source_target_pairs={{0,3},{1,0},{2,1},{3,2},{4,5},{5,6},{6,7},{7,4},{64,67},{65,64},{6... | collective-permute-start | bytes 393224 | tf_op jit(solution)/shard_map/ppermute | solution.py:261
  18.7 7.1 %collective-permute-start.4 = (f32[128,256]{1,0:T(8,128)S(1)}, f32[128,256]{1,0:T(8,128)S(1)}, u32[]{:S(2)}, u32[]{:S(2)}) collective-permute-start(f32[128,256]{1,0:T(8,128)S(1)} %get-tuple-element.27), channel_id=1, source_target_pairs={{0,132},{4,128},{8,140},{12,136},{16,148},{20,144},{24,156},{28,15... | collective-permute-start | bytes 393224 | tf_op jit(solution)/shard_map/ppermute | solution.py:266
  21.5 7.7 %collective-permute-start.5 = (f32[128,256]{1,0:T(8,128)S(1)}, f32[128,256]{1,0:T(8,128)S(1)}, u32[]{:S(2)}, u32[]{:S(2)}) collective-permute-start(f32[128,256]{1,0:T(8,128)S(1)} %get-tuple-element.28), channel_id=1, source_target_pairs={{0,196},{4,68},{8,204},{12,76},{16,212},{20,84},{24,220},{28,92},{... | collective-permute-start | bytes 393224 | tf_op jit(solution)/shard_map/ppermute | solution.py:266
  22.7 6.5 %collective-permute-start.6 = (f32[128,256]{1,0:T(8,128)S(1)}, f32[128,256]{1,0:T(8,128)S(1)}, u32[]{:S(2)}, u32[]{:S(2)}) collective-permute-start(f32[128,256]{1,0:T(8,128)S(1)} %get-tuple-element.29), channel_id=1, source_target_pairs={{0,64},{4,192},{8,72},{12,200},{16,80},{20,208},{24,88},{28,216},{... | collective-permute-start | bytes 393224 | tf_op jit(solution)/shard_map/ppermute | solution.py:266
  29.9 14.5 %all-to-all-start = ((f32[8,16,256]{2,1,0:T(8,128)}), f32[8,16,256]{2,1,0:T(8,128)S(1)}, u32[]{:S(2)}, u32[]{:S(2)}) async-start(f32[8,16,256]{2,1,0:T(8,128)} %gather.1), calls=%async_computation | async-start | bytes 262144 | tf_op jit(solution)/shard_map/all_to_all | solution.py:268
